TPU v7x, 256 devices: a whole 4x4x8 slice. The times are simulated.
256 devices in a mesh: azim: 32 (over z, y_lo, core), rad: 4 (over x), axial: 2 (over y_hi).
Axes of the slice: x: 4, y: 4 (y_hi: 2, y_lo: 2; y = y_hi * 2 + y_lo), z: 8, core: 2. Of those that a mesh axis runs over, the one named last changes fastest.
Arguments:
- adjoint_final: float32 [4, 48, 64, 8, 512], P(None, None, 'azim', 'axial', 'rad'), may hold values from -6 to 6
- state_start: bfloat16 [4, 48, 64, 8, 512], P(None, None, 'azim', 'axial', 'rad'), may hold values from 0.099609375 to 2
- state_middle: bfloat16 [4, 48, 64, 8, 512], P(None, None, 'azim', 'axial', 'rad'), may hold values from 0.099609375 to 2
- speeds: float32 [3, 64, 8, 512], P(None, 'azim', 'axial', 'rad'), may hold values from 0.04 to 0.25
- flags: int32 [3, 64, 8, 512], P(None, 'azim', 'axial', 'rad'), may hold values from 0 to 1
- zones: int32 [64, 8, 512], P('azim', 'axial', 'rad'), may hold values from 0 to 3
- growth_rate: float32 [48], replicated, may hold values from 0.05 to 0.5
- transfer_rate: float32 [48], replicated, may hold values from 0.05 to 0.5
- nucleation_rate: float32 [4], replicated, may hold values from 0.2 to 1
Outputs:
- adjoint_start: float32 [4, 48, 64, 8, 512], P(None, None, 'azim', 'axial', 'rad')
All inputs are finite; a program needn't handle non-finite values.
Results may differ from a plain program's by a relative error of at most 0.0003.
Values sent between devices are 32-bit elements; how exact they have to be, the bound alone decides.
A program may use at most 128 MiB of HBM per device.

v0:
```python
import jax
import jax.numpy as jnp
from jax import lax
from jax.sharding import PartitionSpec as P

supersat_scale = 1.5
crowding = 0.02
nucleus_moments = (1.0, 0.5, 0.25, 0.125)


def extended(x, sides, width, wrap):
    for axis, dim in sides:
        size, length = (lax.axis_size(axis), x.shape[dim])
        up = [(i, (i + 1) % size) for i in range(size if wrap else size - 1)]
        down = [(j, i) for i, j in up]
        last = lax.slice_in_dim(x, length - width, length, axis=dim)
        first = lax.slice_in_dim(x, 0, width, axis=dim)
        before = lax.ppermute(last, axis, up)
        after = lax.ppermute(first, axis, down)
        x = jnp.concatenate([before, x, after], axis=dim)
    return x


def source_term(state, growth_rate, transfer_rate, nucleation):
    extra = (1,) * (state.ndim - 2)
    growth = growth_rate.reshape((1, -1) + extra)
    transfer = transfer_rate.reshape((1, -1) + extra)
    third = state[3]
    sigma = supersat_scale / (1.0 + crowding * jnp.sum(third * third, axis=0))
    lower = jnp.concatenate([jnp.zeros_like(state[0:1]), state[:3]], axis=0)
    factors = jnp.array([0.0, 1.0, 2.0, 3.0], dtype=state.dtype).reshape((4, 1) + extra)
    outflow = transfer * state
    inflow = jnp.concatenate([jnp.zeros_like(outflow[:, 0:1]), outflow[:, :-1]], axis=1)
    first = (jnp.arange(state.shape[1]) == 0).astype(state.dtype).reshape((1, -1) + extra)
    nucleus = jnp.array(nucleus_moments, dtype=state.dtype).reshape((4, 1) + extra)
    birth = nucleus * first * (nucleation * sigma * sigma)[None, None]
    return sigma[None, None] * (factors * growth * lower + inflow - outflow) + birth


def source_adjoint(state, adjoint, growth_rate, transfer_rate, nucleation):
    _, pull = jax.vjp(
        lambda field: source_term(field, growth_rate, transfer_rate, nucleation), state
    )
    return pull(adjoint)[0]


def cut_region(field, direction, offset):
    lead = [slice(None)] * (field.ndim - 3)
    spatial = []
    for which in range(3):
        moved = offset if which == direction else 0
        length = field.shape[field.ndim - 3 + which]
        spatial.append(slice(1 + moved, length - 1 + moved))
    return field[tuple(lead + spatial)]


def transport_adjoint(adjoint_pad, coeff_pad):
    total = None
    for direction in range(3):
        centre = cut_region(adjoint_pad, direction, 0)
        higher = cut_region(adjoint_pad, direction, 1)
        lowerv = cut_region(adjoint_pad, direction, -1)
        p_high = cut_region(coeff_pad[direction], direction, 1)
        q_here = cut_region(coeff_pad[3 + direction], direction, 0)
        term = p_high * (higher - centre) + q_here * (lowerv - centre)
        total = term if total is None else total + term
    return total


def face_coefficients(speeds, flags):
    upwind = flags.astype(speeds.dtype)
    return jnp.concatenate([speeds * upwind, speeds * (1.0 - upwind)], axis=0)


def nucleation_field(zones, nucleation_rate):
    labels = jnp.arange(nucleation_rate.shape[0], dtype=jnp.int32).reshape((-1, 1, 1, 1))
    match = (zones[None] == labels).astype(nucleation_rate.dtype)
    return jnp.sum(match * nucleation_rate.reshape((-1, 1, 1, 1)), axis=0)


def shards(
    adjoint_final,
    state_start,
    state_middle,
    speeds,
    flags,
    zones,
    growth_rate,
    transfer_rate,
    nucleation_rate,
):
    coeffs = face_coefficients(speeds, flags)
    nucleation = nucleation_field(zones, nucleation_rate)
    start = state_start.astype(jnp.float32)
    middle = state_middle.astype(jnp.float32)
    dims = adjoint_final.shape
    comps = dims[0] * dims[1]
    packed = jnp.concatenate([adjoint_final.reshape((comps,) + dims[2:]), coeffs], axis=0)
    packed = extended(packed, (("azim", 1),), 1, True)
    packed = extended(packed, (("rad", 3), ("axial", 2)), 1, False)
    later_pad = packed[:comps].reshape(dims[:2] + packed.shape[1:])
    coeff_pad = packed[comps:]
    adjoint_middle = 0.5 * adjoint_final + 0.5 * (
        transport_adjoint(later_pad, coeff_pad)
        + source_adjoint(middle, adjoint_final, growth_rate, transfer_rate, nucleation)
    )
    flat = adjoint_middle.reshape((comps,) + dims[2:])
    flat = extended(flat, (("azim", 1),), 1, True)
    flat = extended(flat, (("rad", 3), ("axial", 2)), 1, False)
    middle_pad = flat.reshape(dims[:2] + flat.shape[1:])
    return (
        0.5 * adjoint_final
        + adjoint_middle
        + transport_adjoint(middle_pad, coeff_pad)
        + source_adjoint(start, adjoint_middle, growth_rate, transfer_rate, nucleation)
    )


def solution(mesh):
    return jax.shard_map(
        shards,
        mesh=mesh,
        in_specs=(
            P(None, None, "azim", "axial", "rad"),
            P(None, None, "azim", "axial", "rad"),
            P(None, None, "azim", "axial", "rad"),
            P(None, "azim", "axial", "rad"),
            P(None, "azim", "axial", "rad"),
            P("azim", "axial", "rad"),
            P(),
            P(),
            P(),
        ),
        out_specs=P(None, None, "azim", "axial", "rad"),
        check_vma=False,
    )
```

profile of v0, /device:TPU:145, one launch (start us, length us, event | category | flops | bytes accessed | tf_op | source)
XLA Modules:
  0.0 140.1 jit_solution(2101906072826138179)
XLA Ops:
  0.0 1.1 copy_convert_fusion.1
  1.2 0.8 copy-done.2
  2.2 0.2 copy-done.6
  2.4 0.1 broadcast_multiply_fusion.3
  2.6 0.2 copy-done.31
  2.9 0.2 copy-done.1
  3.1 0.5 copy-done
  3.5 1.6 %fusion.35 = (f32[4,48,2,4,128]{4,1,0,3,2:T(8,128)S(1)}, f32[4,48,2,4,128]{4,1,0,3,2:T(8,128)}, f32[2,4,128]{2,1,0:T(4,128)S(1)}, f32[2,4,128]{2,1,0:T(4,128)S(1)}, f32[4,48,2,4,128]{4,1,0,3,2:T(8,128)}) fusion(f32[4,48,2,4,128]{4,3,2,1,0:T(4,128)S(1)} %copy-done, f32[2,4,128]{2,1,0:T(4,128)S(1)} %get-tuple-element.38, f32[4,48]{1,0:T(4,128)S(1)} %get-tuple-element.37, ...), kind=kLoop, calls=%fused_computation.98 | loop fusion | flops 2357248 | bytes 5306048 | tf_op args[0]
  5.3 0.8 collective-permute-start.1
  6.1 1.1 collective-permute-start
  7.2 9.9 %collective-permute-done.1 = f32[198,1,4,128]{3,0,2,1:T(8,128)S(1)} collective-permute-done((f32[198,1,4,128]{3,0,2,1:T(8,128)S(1)}, f32[198,1,4,128]{3,0,2,1:T(8,128)S(1)}, u32[]{:S(2)}, u32[]{:S(2)}) %collective-permute-start.1) | collective-permute-done | bytes 405536 | tf_op jit(solution)/shard_map/ppermute | solution.py:19
  17.2 0.7 copy-done.3
  17.9 0.7 copy-done.4
  18.6 0.2 pad_maximum_fusion.2
  18.8 1.7 %fusion.31 = (f32[198,4,4,1]{3,0,2,1:T(8,128)S(1)}, f32[198,4,4,1]{3,0,2,1:T(8,128)}) fusion(f32[198,4,4,128]{3,0,2,1:T(8,128)S(1)} %pad_maximum_fusion.2), kind=kLoop, calls=%fused_computation.94 | loop fusion | bytes 50688 | tf_op jit(solution)/shard_map/slice | solution.py:16
  20.5 2.0 %copy.130 = f32[198,4,4,1]{0,2,3,1:T(4,128)S(1)} copy(f32[198,4,4,1]{3,0,2,1:T(8,128)} %get-tuple-element.22) | data formatting | bytes 25344 | tf_op jit(solution)/shard_map/slice | solution.py:17
  22.6 1.3 collective-permute-start.3
  23.9 0.6 copy.129
  24.5 4.0 %collective-permute-start.2 = (f32[198,4,4,1]{0,2,3,1:T(4,128)S(1)}, f32[198,4,4,1]{0,2,3,1:T(4,128)S(1)}, u32[]{:S(2)}, u32[]{:S(2)}) collective-permute-start(f32[198,4,4,1]{0,2,3,1:T(4,128)S(1)} %copy.129), channel_id=1, source_target_pairs={{0,2},{2,4},{4,6},{1,3},{3,5},{5,7},{8,10},{10,12},{12,14},{9,11},... | collective-permute-start | bytes 38024 | tf_op jit(solution)/shard_map/ppermute | solution.py:18
  28.6 2.1 %split.16 = f32[4,47,2,4,128]{4,1,0,3,2:T(8,128)} slice(f32[4,48,2,4,128]{4,1,0,3,2:T(8,128)} %get-tuple-element.30), slice={[0:4], [1:48], [0:2], [0:4], [0:128]} | slice | bytes 1540096 | tf_op jit(solution)/shard_map/transpose(jvp())/split | solution.py:33
  30.7 0.5 copy.132
  31.2 1.8 %copy.131 = f32[198,4,4,1]{3,0,2,1:T(8,128)} copy(f32[198,4,4,1]{0,2,3,1:T(4,128)S(1)} %collective-permute-done.2) | data formatting | bytes 25344 | tf_op jit(solution)/shard_map/ppermute | solution.py:18
  33.0 3.1 %pad_maximum_fusion.10 = (f32[198,4,1,130]{3,0,2,1:T(8,128)}, f32[198,4,1,130]{3,0,2,1:T(8,128)}) fusion(f32[198,4,4,1]{3,0,2,1:T(8,128)S(1)} %copy.132, f32[198,4,4,1]{3,0,2,1:T(8,128)} %copy.131, f32[198,1,4,128]{3,0,2,1:T(8,128)} %copy-done.3, f32[198,1,4,128]{3,0,2,1:T(8,128)} %copy-done.4, f32[3,2,4,128]{3,0,2,1:T(4,128)S(1)} %copy.128, ...), kind=kLoop, calls=%fused_computation.10 | loop fusion | flops 1235520 | bytes 2471040 | tf_op jit(solution)/shard_map/slice | solution.py:16
  36.1 2.3 %copy.134 = f32[198,4,1,130]{0,1,3,2:T(4,128)} copy(f32[198,4,1,130]{3,0,2,1:T(8,128)} %get-tuple-element.18) | data formatting | bytes 823680 | tf_op jit(solution)/shard_map/slice | solution.py:17
  38.4 2.9 %collective-permute-start.5 = (f32[198,4,1,130]{0,1,3,2:T(4,128)}, f32[198,4,1,130]{0,1,3,2:T(4,128)}, u32[]{:S(2)}, u32[]{:S(2)}) collective-permute-start(f32[198,4,1,130]{0,1,3,2:T(4,128)} %copy.134), channel_id=1, source_target_pairs={{1,0},{3,2},{5,4},{7,6},{9,8},{11,10},{13,12},{15,14},{17,16},{19,... | collective-permute-start | bytes 1235528 | tf_op jit(solution)/shard_map/ppermute | solution.py:19
  41.3 2.3 %copy.133 = f32[198,4,1,130]{0,1,3,2:T(4,128)} copy(f32[198,4,1,130]{3,0,2,1:T(8,128)} %get-tuple-element.17) | data formatting | bytes 823680 | tf_op jit(solution)/shard_map/slice | solution.py:16
  43.6 1.3 collective-permute-start.4
  44.8 1.0 add_multiply_fusion.1
  45.8 2.0 %slice_multiply_fusion.1 = f32[3,48,2,4,128]{4,1,0,3,2:T(8,128)} fusion(f32[4,48,2,4,128]{4,1,0,3,2:T(8,128)} %get-tuple-element.30, f32[3,48]{1,0:T(4,128)S(1)} %slice.228), kind=kLoop, calls=%fused_computation.61 | loop fusion | flops 147456 | bytes 1180224 | tf_op jit(solution)/shard_map/transpose(jvp())/mul | solution.py:37
  47.8 4.1 %collective-permute-done.5 = f32[198,4,1,130]{0,1,3,2:T(4,128)} collective-permute-done((f32[198,4,1,130]{0,1,3,2:T(4,128)}, f32[198,4,1,130]{0,1,3,2:T(4,128)}, u32[]{:S(2)}, u32[]{:S(2)}) %collective-permute-start.5) | collective-permute-done | bytes 411872 | tf_op jit(solution)/shard_map/ppermute | solution.py:19
  51.9 2.3 %copy.136 = f32[198,4,1,130]{3,0,2,1:T(8,128)} copy(f32[198,4,1,130]{0,1,3,2:T(4,128)} %collective-permute-done.5) | data formatting | bytes 823680 | tf_op jit(solution)/shard_map/ppermute | solution.py:19
  54.2 6.4 %collective-permute-done.4 = f32[198,4,1,130]{0,1,3,2:T(4,128)} collective-permute-done((f32[198,4,1,130]{0,1,3,2:T(4,128)}, f32[198,4,1,130]{0,1,3,2:T(4,128)}, u32[]{:S(2)}, u32[]{:S(2)}) %collective-permute-start.4) | collective-permute-done | bytes 411872 | tf_op jit(solution)/shard_map/ppermute | solution.py:18
  60.6 2.3 %copy.135 = f32[198,4,1,130]{3,0,2,1:T(8,128)} copy(f32[198,4,1,130]{0,1,3,2:T(4,128)} %collective-permute-done.4) | data formatting | bytes 823680 | tf_op jit(solution)/shard_map/ppermute | solution.py:18
  62.9 6.8 %pad_maximum_fusion = f32[198,4,6,130]{3,0,2,1:T(8,128)S(1)} fusion(f32[198,4,1,130]{3,0,2,1:T(8,128)} %copy.136, f32[198,4,4,1]{3,0,2,1:T(8,128)S(1)} %copy.132, f32[198,1,4,128]{3,0,2,1:T(8,128)} %copy-done.3, f32[3,2,4,128]{3,0,2,1:T(4,128)S(1)} %copy.128, f32[3,2,4,128]{3,0,2,1:T(4,128)S(1)} %copy.127, f32[192,2,4,128]{3,0,2,1:T(8,128)S(1)} %bitcast.33, ...), kind=kLoop, calls=%fused_computation | loop fusion | flops 4942080 | bytes 4942080 | tf_op jit(solution)/shard_map/concatenate | solution.py:20
  69.7 0.6 slice.209
  71.0 2.2 %broadcast_multiply_fusion = (f32[4,48,2,4,128]{4,1,0,3,2:T(8,128)}, f32[4,48,2,4,128]{4,1,0,3,2:T(8,128)S(1)}) fusion(f32[2,4,128]{2,1,0:T(4,128)S(1)} %get-tuple-element.39, f32[1,48,2,4,128]{4,1,0,3,2:T(8,128)S(1)} %add_multiply_fusion.1, f32[3,48,2,4,128]{4,1,0,3,2:T(8,128)S(1)} %copy-done.12, f32[4,47,2,4,128]{4,1,0,3,2:T(8,128)S(1)} %copy-done.9, ...), kind=kLoop, calls=%fused_computation.64 | loop fusion | flops 5505024 | bytes 9453760 | tf_op jit(solution)/shard_map/transpose(jvp())/mul | solution.py:37
  73.3 0.5 collective-permute-start.7
  73.8 1.5 %collective-permute-start.6 = (f32[192,1,4,128]{3,0,2,1:T(8,128)S(1)}, f32[192,1,4,128]{3,0,2,1:T(8,128)S(1)}, u32[]{:S(2)}, u32[]{:S(2)}) collective-permute-start(f32[192,1,4,128]{3,0,2,1:T(8,128)S(1)} %get-tuple-element.27), channel_id=1, source_target_pairs={{0,8},{8,16},{16,24},{24,32},{32,40},{40,48},{48,56},{56,64},{64,7... | collective-permute-start | bytes 1179656 | tf_op jit(solution)/shard_map/ppermute | solution.py:18
  75.4 1.0 multiply_reduce_fusion.1
  76.4 8.6 %collective-permute-done.7 = f32[192,1,4,128]{3,0,2,1:T(8,128)S(1)} collective-permute-done((f32[192,1,4,128]{3,0,2,1:T(8,128)S(1)}, f32[192,1,4,128]{3,0,2,1:T(8,128)S(1)}, u32[]{:S(2)}, u32[]{:S(2)}) %collective-permute-start.7) | collective-permute-done | bytes 393248 | tf_op jit(solution)/shard_map/ppermute | solution.py:19
  85.0 0.7 copy-done.5
  85.9 1.7 %fusion.32 = (f32[192,4,4,1]{3,0,2,1:T(8,128)S(1)}, f32[192,4,4,1]{3,0,2,1:T(8,128)}) fusion(f32[192,4,4,128]{3,0,2,1:T(8,128)S(1)} %pad_maximum_fusion.3), kind=kLoop, calls=%fused_computation.95 | loop fusion | bytes 49152 | tf_op jit(solution)/shard_map/slice | solution.py:16
  87.6 2.6 %copy.154 = f32[192,4,4,1]{0,2,3,1:T(4,128)} copy(f32[192,4,4,1]{3,0,2,1:T(8,128)} %get-tuple-element.24) | data formatting | bytes 24576 | tf_op jit(solution)/shard_map/slice | solution.py:17
  90.2 1.3 collective-permute-start.9
  91.5 1.2 copy.153
  92.7 4.6 %collective-permute-start.8 = (f32[192,4,4,1]{0,2,3,1:T(4,128)}, f32[192,4,4,1]{0,2,3,1:T(4,128)}, u32[]{:S(2)}, u32[]{:S(2)}) collective-permute-start(f32[192,4,4,1]{0,2,3,1:T(4,128)} %copy.153), channel_id=1, source_target_pairs={{0,2},{2,4},{4,6},{1,3},{3,5},{5,7},{8,10},{10,12},{12,14},{9,11},... | collective-permute-start | bytes 36872 | tf_op jit(solution)/shard_map/ppermute | solution.py:18
  97.3 1.3 negate_multiply_fusion
  98.6 2.1 %split.18 = f32[4,47,2,4,128]{4,1,0,3,2:T(8,128)} slice(f32[4,48,2,4,128]{4,1,0,3,2:T(8,128)} %get-tuple-element.9), slice={[0:4], [1:48], [0:2], [0:4], [0:128]} | slice | bytes 1540096 | tf_op jit(solution)/shard_map/transpose(jvp())/split | solution.py:33
  100.7 1.2 copy.156
  101.9 2.4 %copy.155 = f32[192,4,4,1]{3,0,2,1:T(8,128)} copy(f32[192,4,4,1]{0,2,3,1:T(4,128)} %collective-permute-done.8) | data formatting | bytes 24576 | tf_op jit(solution)/shard_map/ppermute | solution.py:18
  104.3 3.0 %pad_maximum_fusion.16 = (f32[192,4,1,130]{3,0,2,1:T(8,128)}, f32[192,4,1,130]{3,0,2,1:T(8,128)}) fusion(f32[192,4,4,1]{3,0,2,1:T(8,128)S(1)} %copy.156, f32[192,4,4,1]{3,0,2,1:T(8,128)} %copy.155, f32[192,1,4,128]{3,0,2,1:T(8,128)S(1)} %collective-permute-done.7, f32[192,2,4,128]{3,0,2,1:T(8,128)S(1)} %bitcast.26, f32[192,1,4,128]{3,0,2,1:T(8,128)} %copy-done.5), kind=kLoop, calls=%fused_computation.35 | loop fusion | flops 798720 | bytes 2396160 | tf_op jit(solution)/shard_map/slice | solution.py:16
  107.3 2.3 %copy.158 = f32[192,4,1,130]{0,1,3,2:T(4,128)} copy(f32[192,4,1,130]{3,0,2,1:T(8,128)} %get-tuple-element.20) | data formatting | bytes 798720 | tf_op jit(solution)/shard_map/slice | solution.py:17
  109.6 2.3 %collective-permute-start.11 = (f32[192,4,1,130]{0,1,3,2:T(4,128)}, f32[192,4,1,130]{0,1,3,2:T(4,128)}, u32[]{:S(2)}, u32[]{:S(2)}) collective-permute-start(f32[192,4,1,130]{0,1,3,2:T(4,128)} %copy.158), channel_id=1, source_target_pairs={{1,0},{3,2},{5,4},{7,6},{9,8},{11,10},{13,12},{15,14},{17,16},{19,... | collective-permute-start | bytes 1198088 | tf_op jit(solution)/shard_map/ppermute | solution.py:19
  111.9 2.3 %copy.157 = f32[192,4,1,130]{0,1,3,2:T(4,128)} copy(f32[192,4,1,130]{3,0,2,1:T(8,128)} %get-tuple-element.19) | data formatting | bytes 798720 | tf_op jit(solution)/shard_map/slice | solution.py:16
  114.1 1.3 collective-permute-start.10
  115.4 1.6 %add_multiply_fusion = f32[1,48,2,4,128]{4,1,0,3,2:T(8,128)} fusion(f32[4,48,2,4,128]{4,1,0,3,2:T(8,128)} %copy-done.1, f32[2,4,128]{2,1,0:T(4,128)} %negate_multiply_fusion), kind=kLoop, calls=%fused_computation.68 | loop fusion | flops 98304 | bytes 397312 | tf_op jit(solution)/shard_map/transpose(jvp())/add_any | solution.py:29
  117.0 2.0 %slice_multiply_fusion = f32[3,48,2,4,128]{4,1,0,3,2:T(8,128)} fusion(f32[4,48,2,4,128]{4,1,0,3,2:T(8,128)} %get-tuple-element.9, f32[3,48]{1,0:T(4,128)} %copy-done.25), kind=kLoop, calls=%fused_computation.60 | loop fusion | flops 147456 | bytes 1180224 | tf_op jit(solution)/shard_map/transpose(jvp())/mul | solution.py:37
  119.0 3.3 %collective-permute-done.11 = f32[192,4,1,130]{0,1,3,2:T(4,128)} collective-permute-done((f32[192,4,1,130]{0,1,3,2:T(4,128)}, f32[192,4,1,130]{0,1,3,2:T(4,128)}, u32[]{:S(2)}, u32[]{:S(2)}) %collective-permute-start.11) | collective-permute-done | bytes 399392 | tf_op jit(solution)/shard_map/ppermute | solution.py:19
  122.3 2.3 %copy.160 = f32[192,4,1,130]{3,0,2,1:T(8,128)} copy(f32[192,4,1,130]{0,1,3,2:T(4,128)} %collective-permute-done.11) | data formatting | bytes 798720 | tf_op jit(solution)/shard_map/ppermute | solution.py:19
  124.6 6.4 %collective-permute-done.10 = f32[192,4,1,130]{0,1,3,2:T(4,128)} collective-permute-done((f32[192,4,1,130]{0,1,3,2:T(4,128)}, f32[192,4,1,130]{0,1,3,2:T(4,128)}, u32[]{:S(2)}, u32[]{:S(2)}) %collective-permute-start.10) | collective-permute-done | bytes 399392 | tf_op jit(solution)/shard_map/ppermute | solution.py:18
  131.0 2.3 %copy.159 = f32[192,4,1,130]{3,0,2,1:T(8,128)} copy(f32[192,4,1,130]{0,1,3,2:T(4,128)} %collective-permute-done.10) | data formatting | bytes 798720 | tf_op jit(solution)/shard_map/ppermute | solution.py:18
  133.3 3.9 %pad_maximum_fusion.1 = f32[192,4,6,130]{3,0,2,1:T(8,128)S(1)} fusion(f32[192,4,1,130]{3,0,2,1:T(8,128)} %copy.160, f32[192,4,4,1]{3,0,2,1:T(8,128)S(1)} %copy.156, f32[192,1,4,128]{3,0,2,1:T(8,128)S(1)} %collective-permute-done.7, f32[192,2,4,128]{3,0,2,1:T(8,128)S(1)} %bitcast.27, f32[192,1,4,128]{3,0,2,1:T(8,128)} %copy-done.5, ...), kind=kLoop, calls=%fused_computation.1 | loop fusion | flops 3594240 | bytes 4792320 | tf_op jit(solution)/shard_map/concatenate | solution.py:20
  137.2 1.4 %fusion.4 = f32[4,48,2,4,128]{4,1,0,3,2:T(8,128)S(1)} fusion(f32[4,48,4,6,130]{4,1,0,3,2:T(8,128)S(1)} %bitcast.29, f32[1,48,2,4,128]{4,1,0,3,2:T(8,128)S(1)} %copy-done.14, f32[3,48,2,4,128]{4,1,0,3,2:T(8,128)S(1)} %copy-done.13, f32[4,47,2,4,128]{4,1,0,3,2:T(8,128)S(1)} %copy-done.10, f32[4,48,2,4,128]{4,1,0,3,2:T(8,128)S(1)} %get-tuple-element.10, ...), kind=kLoop, calls=%fused_computation.17 | loop fusion | flops 5308416 | bytes 9449664 | tf_op jit(solution)/shard_map/add | solution.py:112
  138.7 1.4 copy.162
  (110 shorter events, 1.4 us)
Async XLA Ops:
  0.0 2.1 %copy-start.7 = (bf16[4,48,2,4,128]{4,3,2,1,0:T(4,128)(2,1)S(1)}, bf16[4,48,2,4,128]{4,3,2,1,0:T(4,128)(2,1)}, u32[]{:S(2)}) copy-start(bf16[4,48,2,4,128]{4,3,2,1,0:T(4,128)(2,1)} %param.14) | copy-start | bytes 1179652
  1.1 0.9 copy-start.2
  1.1 1.3 copy-start.6
  1.1 1.3 copy-start.28
  2.0 0.7 copy-start.31
  2.0 0.8 copy-start.32
  2.1 0.7 copy-start.35
  2.1 0.7 copy-start.36
  2.1 1.5 %copy-start = (f32[4,48,2,4,128]{4,3,2,1,0:T(4,128)S(1)}, f32[4,48,2,4,128]{4,3,2,1,0:T(4,128)}, u32[]{:S(2)}) copy-start(f32[4,48,2,4,128]{4,3,2,1,0:T(4,128)} %param.13) | copy-start | bytes 2359300
  2.2 0.9 copy-start.1
  2.4 0.7 copy-start.22
  2.8 68.1 %copy-start.19 = (f32[2,4,128]{2,1,0:T(4,128)}, f32[2,4,128]{2,1,0:T(4,128)S(1)}, u32[]{:S(2)}) copy-start(f32[2,4,128]{2,1,0:T(4,128)S(1)} %get-tuple-element.39) | copy-start | bytes 12292
  2.9 2.3 %copy-start.26 = (f32[4,48]{1,0:T(4,128)}, f32[4,48]{1,0:T(4,128)S(1)}, u32[]{:S(2)}) copy-start(f32[4,48]{1,0:T(4,128)S(1)} %get-tuple-element.37) | copy-start | bytes 2308
  2.9 25.6 %copy-start.23 = (f32[4,48]{1,0:T(4,128)}, f32[4,48]{1,0:T(4,128)S(1)}, u32[]{:S(2)}) copy-start(f32[4,48]{1,0:T(4,128)S(1)} %get-tuple-element.36) | copy-start | bytes 2308
  5.2 2.0 %copy-start.33 = (s32[2,4,128]{2,1,0:T(4,128)S(1)}, s32[2,4,128]{2,1,0:T(4,128)}, u32[]{:S(2)}) copy-start(s32[2,4,128]{2,1,0:T(4,128)} %param.18) | copy-start | bytes 12292
  5.2 2.0 %copy-start.34 = (f32[4]{0:T(128)S(1)}, f32[4]{0:T(128)}, u32[]{:S(2)}) copy-start(f32[4]{0:T(128)} %param.21) | copy-start | bytes 52
  5.3 11.8 %collective-permute-start.1 = (f32[198,1,4,128]{3,0,2,1:T(8,128)S(1)}, f32[198,1,4,128]{3,0,2,1:T(8,128)S(1)}, u32[]{:S(2)}, u32[]{:S(2)}) collective-permute-start(f32[198,1,4,128]{3,0,2,1:T(8,128)S(1)} %get-tuple-element.26), channel_id=1, source_target_pairs={{8,0},{16,8},{24,16},{32,24},{40,32},{48,40},{56,48},{64,56},{72,6... | collective-permute-start | bytes 1216520 | tf_op jit(solution)/shard_map/ppermute | solution.py:19
  6.1 11.1 %collective-permute-start = (f32[198,1,4,128]{3,0,2,1:T(8,128)S(1)}, f32[198,1,4,128]{3,0,2,1:T(8,128)S(1)}, u32[]{:S(2)}, u32[]{:S(2)}) collective-permute-start(f32[198,1,4,128]{3,0,2,1:T(8,128)S(1)} %get-tuple-element.25), channel_id=1, source_target_pairs={{0,8},{8,16},{16,24},{24,32},{32,40},{40,48},{48,56},{56,64},{64,7... | collective-permute-start | bytes 1216520 | tf_op jit(solution)/shard_map/ppermute | solution.py:18
  7.2 21.3 %copy-start.21 = (f32[2,4,128]{2,1,0:T(4,128)}, f32[2,4,128]{2,1,0:T(4,128)S(1)}, u32[]{:S(2)}) copy-start(f32[2,4,128]{2,1,0:T(4,128)S(1)} %select_reduce_fusion) | copy-start | bytes 12292
  17.2 0.8 copy-start.3
  17.9 0.7 copy-start.4
  22.6 8.1 %collective-permute-start.3 = (f32[198,4,4,1]{0,2,3,1:T(4,128)S(1)}, f32[198,4,4,1]{0,2,3,1:T(4,128)S(1)}, u32[]{:S(2)}, u32[]{:S(2)}) collective-permute-start(f32[198,4,4,1]{0,2,3,1:T(4,128)S(1)} %copy.130), channel_id=1, source_target_pairs={{2,0},{4,2},{6,4},{3,1},{5,3},{7,5},{10,8},{12,10},{14,12},{11,9},... | collective-permute-start | bytes 38024 | tf_op jit(solution)/shard_map/ppermute | solution.py:19
  24.5 6.7 %collective-permute-start.2 = (f32[198,4,4,1]{0,2,3,1:T(4,128)S(1)}, f32[198,4,4,1]{0,2,3,1:T(4,128)S(1)}, u32[]{:S(2)}, u32[]{:S(2)}) collective-permute-start(f32[198,4,4,1]{0,2,3,1:T(4,128)S(1)} %copy.129), channel_id=1, source_target_pairs={{0,2},{2,4},{4,6},{1,3},{3,5},{5,7},{8,10},{10,12},{12,14},{9,11},... | collective-permute-start | bytes 38024 | tf_op jit(solution)/shard_map/ppermute | solution.py:18
  28.6 17.2 %copy-start.25 = (f32[3,48]{1,0:T(4,128)}, f32[3,48]{1,0:T(4,128)S(1)}, u32[]{:S(2)}) copy-start(f32[3,48]{1,0:T(4,128)S(1)} %slice.228) | copy-start | bytes 1732
  38.4 13.5 %collective-permute-start.5 = (f32[198,4,1,130]{0,1,3,2:T(4,128)}, f32[198,4,1,130]{0,1,3,2:T(4,128)}, u32[]{:S(2)}, u32[]{:S(2)}) collective-permute-start(f32[198,4,1,130]{0,1,3,2:T(4,128)} %copy.134), channel_id=1, source_target_pairs={{1,0},{3,2},{5,4},{7,6},{9,8},{11,10},{13,12},{15,14},{17,16},{19,... | collective-permute-start | bytes 1235528 | tf_op jit(solution)/shard_map/ppermute | solution.py:19
  43.6 17.0 %collective-permute-start.4 = (f32[198,4,1,130]{0,1,3,2:T(4,128)}, f32[198,4,1,130]{0,1,3,2:T(4,128)}, u32[]{:S(2)}, u32[]{:S(2)}) collective-permute-start(f32[198,4,1,130]{0,1,3,2:T(4,128)} %copy.133), channel_id=1, source_target_pairs={{0,1},{2,3},{4,5},{6,7},{8,9},{10,11},{12,13},{14,15},{16,17},{18,... | collective-permute-start | bytes 1235528 | tf_op jit(solution)/shard_map/ppermute | solution.py:18
  69.7 1.3 copy-start.9
  69.7 1.3 copy-start.12
  70.9 2.4 %copy-start.15 = (f32[2,4,128]{2,1,0:T(4,128)}, f32[2,4,128]{2,1,0:T(4,128)S(1)}, u32[]{:S(2)}) copy-start(f32[2,4,128]{2,1,0:T(4,128)S(1)} %copy.140) | copy-start | bytes 12292
  71.0 2.3 %copy-start.17 = (f32[2,4,128]{2,1,0:T(4,128)}, f32[2,4,128]{2,1,0:T(4,128)S(1)}, u32[]{:S(2)}) copy-start(f32[2,4,128]{2,1,0:T(4,128)S(1)} %copy.138) | copy-start | bytes 12292
  73.2 2.1 %slice-start = ((f32[4,48,2,4,128]{4,1,0,3,2:T(8,128)}), f32[3,48,2,4,128]{4,1,0,3,2:T(8,128)S(1)}, s32[]{:S(2)}) async-start(f32[4,48,2,4,128]{4,1,0,3,2:T(8,128)} %copy-done.1), calls=%async_computation | async-start | bytes 1179648 | tf_op jit(solution)/shard_map/jvp()/slice | solution.py:30
  73.2 2.1 %copy-start.8 = (bf16[4,48,2,4,128]{4,3,2,1,0:T(4,128)(2,1)S(1)}, bf16[4,48,2,4,128]{4,3,2,1,0:T(4,128)(2,1)}, u32[]{:S(2)}) copy-start(bf16[4,48,2,4,128]{4,3,2,1,0:T(4,128)(2,1)} %param.14) | copy-start | bytes 1179652
  73.2 2.1 %copy-start.11 = (f32[4,48,2,4,128]{4,1,0,3,2:T(8,128)S(1)}, f32[4,48,2,4,128]{4,1,0,3,2:T(8,128)}, u32[]{:S(2)}) copy-start(f32[4,48,2,4,128]{4,1,0,3,2:T(8,128)} %get-tuple-element.35) | copy-start | bytes 2359300
  73.2 2.1 %copy-start.24 = (f32[4,48]{1,0:T(4,128)S(1)}, f32[4,48]{1,0:T(4,128)}, u32[]{:S(2)}) copy-start(f32[4,48]{1,0:T(4,128)} %copy-done.23) | copy-start | bytes 2308
  73.2 2.1 %copy-start.27 = (f32[4,48]{1,0:T(4,128)S(1)}, f32[4,48]{1,0:T(4,128)}, u32[]{:S(2)}) copy-start(f32[4,48]{1,0:T(4,128)} %copy-done.26) | copy-start | bytes 2308
  73.3 2.1 %copy-start.29 = (f32[48]{0:T(128)S(1)}, f32[48]{0:T(128)}, u32[]{:S(2)}) copy-start(f32[48]{0:T(128)} %param.20) | copy-start | bytes 580
  73.3 11.7 %collective-permute-start.7 = (f32[192,1,4,128]{3,0,2,1:T(8,128)S(1)}, f32[192,1,4,128]{3,0,2,1:T(8,128)S(1)}, u32[]{:S(2)}, u32[]{:S(2)}) collective-permute-start(f32[192,1,4,128]{3,0,2,1:T(8,128)S(1)} %get-tuple-element.28), channel_id=1, source_target_pairs={{8,0},{16,8},{24,16},{32,24},{40,32},{48,40},{56,48},{64,56},{72,6... | collective-permute-start | bytes 1179656 | tf_op jit(solution)/shard_map/ppermute | solution.py:19
  73.8 11.2 %collective-permute-start.6 = (f32[192,1,4,128]{3,0,2,1:T(8,128)S(1)}, f32[192,1,4,128]{3,0,2,1:T(8,128)S(1)}, u32[]{:S(2)}, u32[]{:S(2)}) collective-permute-start(f32[192,1,4,128]{3,0,2,1:T(8,128)S(1)} %get-tuple-element.27), channel_id=1, source_target_pairs={{0,8},{8,16},{16,24},{24,32},{32,40},{40,48},{48,56},{56,64},{64,7... | collective-permute-start | bytes 1179656 | tf_op jit(solution)/shard_map/ppermute | solution.py:18
  85.0 0.7 copy-start.5
  90.2 10.5 %collective-permute-start.9 = (f32[192,4,4,1]{0,2,3,1:T(4,128)}, f32[192,4,4,1]{0,2,3,1:T(4,128)}, u32[]{:S(2)}, u32[]{:S(2)}) collective-permute-start(f32[192,4,4,1]{0,2,3,1:T(4,128)} %copy.154), channel_id=1, source_target_pairs={{2,0},{4,2},{6,4},{3,1},{5,3},{7,5},{10,8},{12,10},{14,12},{11,9},... | collective-permute-start | bytes 36872 | tf_op jit(solution)/shard_map/ppermute | solution.py:19
  92.7 9.2 %collective-permute-start.8 = (f32[192,4,4,1]{0,2,3,1:T(4,128)}, f32[192,4,4,1]{0,2,3,1:T(4,128)}, u32[]{:S(2)}, u32[]{:S(2)}) collective-permute-start(f32[192,4,4,1]{0,2,3,1:T(4,128)} %copy.153), channel_id=1, source_target_pairs={{0,2},{2,4},{4,6},{1,3},{3,5},{5,7},{8,10},{10,12},{12,14},{9,11},... | collective-permute-start | bytes 36872 | tf_op jit(solution)/shard_map/ppermute | solution.py:18
  109.6 12.8 %collective-permute-start.11 = (f32[192,4,1,130]{0,1,3,2:T(4,128)}, f32[192,4,1,130]{0,1,3,2:T(4,128)}, u32[]{:S(2)}, u32[]{:S(2)}) collective-permute-start(f32[192,4,1,130]{0,1,3,2:T(4,128)} %copy.158), channel_id=1, source_target_pairs={{1,0},{3,2},{5,4},{7,6},{9,8},{11,10},{13,12},{15,14},{17,16},{19,... | collective-permute-start | bytes 1198088 | tf_op jit(solution)/shard_map/ppermute | solution.py:19
  114.1 16.9 %collective-permute-start.10 = (f32[192,4,1,130]{0,1,3,2:T(4,128)}, f32[192,4,1,130]{0,1,3,2:T(4,128)}, u32[]{:S(2)}, u32[]{:S(2)}) collective-permute-start(f32[192,4,1,130]{0,1,3,2:T(4,128)} %copy.157), channel_id=1, source_target_pairs={{0,1},{2,3},{4,5},{6,7},{8,9},{10,11},{12,13},{14,15},{16,17},{18,... | collective-permute-start | bytes 1198088 | tf_op jit(solution)/shard_map/ppermute | solution.py:18
  133.3 3.9 %copy-start.10 = (f32[4,47,2,4,128]{4,1,0,3,2:T(8,128)S(1)}, f32[4,47,2,4,128]{4,1,0,3,2:T(8,128)}, u32[]{:S(2)}) copy-start(f32[4,47,2,4,128]{4,1,0,3,2:T(8,128)} %split.18) | copy-start | bytes 2310148
  133.3 3.9 %copy-start.13 = (f32[3,48,2,4,128]{4,1,0,3,2:T(8,128)S(1)}, f32[3,48,2,4,128]{4,1,0,3,2:T(8,128)}, u32[]{:S(2)}) copy-start(f32[3,48,2,4,128]{4,1,0,3,2:T(8,128)} %slice_multiply_fusion) | copy-start | bytes 1769476
  133.3 3.9 %copy-start.14 = (f32[1,48,2,4,128]{4,1,0,3,2:T(8,128)S(1)}, f32[1,48,2,4,128]{4,1,0,3,2:T(8,128)}, u32[]{:S(2)}) copy-start(f32[1,48,2,4,128]{4,1,0,3,2:T(8,128)} %add_multiply_fusion) | copy-start | bytes 589828
  133.3 3.9 %copy-start.16 = (f32[2,4,128]{2,1,0:T(4,128)S(1)}, f32[2,4,128]{2,1,0:T(4,128)}, u32[]{:S(2)}) copy-start(f32[2,4,128]{2,1,0:T(4,128)} %copy-done.15) | copy-start | bytes 12292
  133.3 3.9 %copy-start.18 = (f32[2,4,128]{2,1,0:T(4,128)S(1)}, f32[2,4,128]{2,1,0:T(4,128)}, u32[]{:S(2)}) copy-start(f32[2,4,128]{2,1,0:T(4,128)} %copy-done.17) | copy-start | bytes 12292
  133.3 3.9 %copy-start.20 = (f32[2,4,128]{2,1,0:T(4,128)S(1)}, f32[2,4,128]{2,1,0:T(4,128)}, u32[]{:S(2)}) copy-start(f32[2,4,128]{2,1,0:T(4,128)} %copy-done.19) | copy-start | bytes 12292
  133.3 3.9 %copy-start.30 = (f32[48]{0:T(128)S(1)}, f32[48]{0:T(128)}, u32[]{:S(2)}) copy-start(f32[48]{0:T(128)} %param.20) | copy-start | bytes 580
where the time goes:
time: 141 us; the launch traced here: 140 us
  local copies, waits for them, and re-layouts  45.2 us (32%)
  waiting for transfers between devices  38.8 us (28%)
  other arithmetic  32.8 us (23%)
  starting transfers between devices  22.7 us (16%)
    ppermute x6, waiting for transfers between devices, extended(): after = lax.ppermute(first, axis, down)  26 us
    ppermute x6, starting transfers between devices, extended(): before = lax.ppermute(last, axis, up)  13.7 us
    ppermute x6, waiting for transfers between devices, extended(): before = lax.ppermute(last, axis, up)  12.8 us
    concatenate x4, other arithmetic, extended(): x = jnp.concatenate([before, x, after], axis=dim)  10.9 us
    slice x8, local copies, waits for them, and re-layouts, extended(): last = lax.slice_in_dim(x, length - width, length, axis=dim)  9.92 us
    slice x4, local copies, waits for them, and re-layouts, extended(): first = lax.slice_in_dim(x, 0, width, axis=dim)  9.22 us
    ppermute x6, starting transfers between devices, extended(): after = lax.ppermute(first, axis, down)  8.99 us
    ppermute x4, local copies, waits for them, and re-layouts, extended(): before = lax.ppermute(last, axis, up)  8.71 us
  transfers between devices with their start and end apart: 12, of which 6 were waited for; matrix products, arithmetic and copies ran while one was open for 18% of the time, Pallas kernels for 0%

commit v1 on v0

v1 whole, which is shorter than its diff:
```python
import functools

import jax
import jax.numpy as jnp
from jax import lax
from jax.experimental import pallas as pl
from jax.experimental.pallas import tpu as pltpu
from jax.sharding import PartitionSpec as P

supersat_scale = 1.5
crowding = 0.02
MESH = pl.DeviceIdType.MESH
F32 = jnp.float32


def rolled(x, shift, axis):
    return pltpu.roll(x, shift, axis)


def shifted(axis, step):
    size = lax.axis_size(axis)
    return {axis: lax.rem(lax.axis_index(axis) + step + size, size)}


def kernel(
    far_ref, af_ref, sm_ref, ss_ref, speeds_ref, flags_ref, zones_ref, growth_ref, transfer_ref, nucl_ref,
    out_ref,
    a_v, b_v, o_v, sm_v, ss_v, sp_v, fl_v, zn_v, g_s, t_s, n_s,
    pz_src, pz_dst,
    az_src, az_one, az_two,
    ax_src1, ax_dst1, ax_src2, ax_dst2,
    rd_src1, rd_dst1, rd_src2, rd_dst2,
    local_sem, send_sem, recv_sem, out_sem,
):
    sections = sm_ref.shape[1]
    above, below = shifted("azim", 1), shifted("azim", -1)
    right, left = shifted("rad", 1), shifted("rad", -1)
    other = shifted("axial", 1)
    first_half = lax.axis_index("axial") == 0

    def remote(n, src, dst, device):
        return pltpu.make_async_remote_copy(
            src_ref=src, dst_ref=dst, send_sem=send_sem.at[n], recv_sem=recv_sem.at[n],
            device_id=device, device_id_type=MESH,
        )

    loads = [
        pltpu.make_async_copy(src, dst, local_sem.at[n])
        for n, (src, dst) in enumerate([
            (speeds_ref, sp_v), (flags_ref, fl_v), (af_ref, a_v.at[:, 0:sections]),
            (zones_ref, zn_v), (growth_ref, g_s), (transfer_ref, t_s), (nucl_ref, n_s),
            (sm_ref, sm_v), (ss_ref, ss_v),
        ])
    ]
    barrier = pltpu.get_barrier_semaphore()
    for device in (above, below, right, left, other):
        pl.semaphore_signal(barrier, inc=1, device_id=device, device_id_type=MESH)
    for copy in loads:
        copy.start()
    pl.semaphore_wait(barrier, 5)

    up1 = remote(0, far_ref.at[:, :, 1], az_one.at[:, :, 0], above)
    down1 = remote(1, far_ref.at[:, :, 0], az_one.at[:, :, 1], below)
    up1.start()
    down1.start()

    row = lax.broadcasted_iota(jnp.int32, (8, 128), 0)
    lane = lax.broadcasted_iota(jnp.int32, (8, 128), 1)
    arow = lax.rem(row, 4)
    edge = jnp.where(first_half, 3, 0)

    def pack_axial(values):
        packed = values[0]
        for k in range(1, 4):
            packed = jnp.where(arow == lax.rem(edge + k, 4), rolled(values[k], k, 0), packed)
        return packed

    def pack_radial(s, values, packs):
        here = lax.shift_right_logical(lane, 1) == s
        return [jnp.where(here, rolled(x, 2 * s + 1, 1), pack) for x, pack in zip(values, packs)]

    zero = jnp.zeros((8, 128), F32)

    loads[0].wait()
    loads[1].wait()
    upwind = fl_v[...].astype(F32)
    speeds = sp_v[...]
    p = speeds * upwind
    q = speeds * (1.0 - upwind)
    pz_src[...] = p[0]
    ax_src1[sections] = p[1]
    rd_src1[4] = p[2]
    pz = remote(2, pz_src, pz_dst, below)
    pz.start()

    loads[2].wait()
    a_v[:, sections] = jnp.zeros((4, 8, 128), F32)
    b_v[:, sections] = jnp.zeros((4, 8, 128), F32)

    def pack_first(s, packs):
        values = [a_v[k, s] for k in range(4)]
        ax_src1[s] = pack_axial(values)
        return pack_radial(s, values, packs)

    packs = lax.fori_loop(0, sections, pack_first, [zero] * 4)
    for k in range(4):
        rd_src1[k] = packs[k]
    ax1 = remote(3, ax_src1, ax_dst1, other)
    rr1 = remote(4, rd_src1, rd_dst1.at[0], right)
    rl1 = remote(5, rd_src1, rd_dst1.at[1], left)
    ax1.start()
    rr1.start()
    rl1.start()

    for copy in loads[3:7]:
        copy.wait()
    zones = zn_v[...]
    nucleation = zero
    for z in range(nucl_ref.shape[0]):
        nucleation = nucleation + jnp.where(zones == z, n_s[z], 0.0)
    loads[7].wait()

    def slope(s, k, values, after):
        t = t_s[s]
        term = t * (after - values[k])
        if k < 3:
            term = term + ((k + 1) * g_s[s]) * values[k + 1]
        return term

    def source_sums(s, values, after, state, sums):
        gain, third = sums
        for k in range(4):
            u = state[k, s].astype(F32)
            gain = gain + u * slope(s, k, values, after[k])
            if k == 3:
                third = third + u * u
        return gain, third

    def source_scalars(sums, first):
        gain, third = sums
        sigma = supersat_scale / (1.0 + crowding * third)
        birth = first[0] + 0.5 * first[1] + 0.25 * first[2] + 0.125 * first[3]
        total = gain + 2.0 * sigma * nucleation * birth
        return sigma, (-2.0 * crowding / supersat_scale) * sigma * sigma * total

    def first_sums(s, sums):
        values = [a_v[k, s] for k in range(4)]
        after = [a_v[k, s + 1] for k in range(4)]
        return source_sums(s, values, after, sm_v, sums)

    sums = lax.fori_loop(0, sections, first_sums, (zero, zero))
    sigma1, third1 = source_scalars(sums, [a_v[k, 0] for k in range(4)])

    ax1.wait_recv()
    rr1.wait_recv()
    rl1.wait_recv()
    p0, p1, p2 = p[0], p[1], p[2]
    q0, q1, q2 = q[0], q[1], q[2]
    c_mid = jnp.where(row < 4, rolled(p0, 4, 0), q0)
    c_up = jnp.where(arow < 3, rolled(p1, 7, 0), 0.0)
    c_low = jnp.where(arow > 0, q1, 0.0)
    far_face = jnp.where(first_half, rolled(ax_dst1[sections], 3, 0), 0.0)
    ax_all = jnp.where(arow == 0, q1, jnp.where(arow == 3, far_face, 0.0))
    ax_halo = jnp.where(arow == edge, ax_all, 0.0)
    c_right = jnp.where(lane < 127, rolled(p2, 127, 1), 0.0)
    c_left = jnp.where(lane > 0, q2, 0.0)
    rad_index = lax.axis_index("rad")
    rad_last = lax.axis_size("rad") - 1
    rd_high = jnp.where(rad_index < rad_last, rolled(rd_dst1[1, 4], 127, 1), 0.0)
    rd_all = jnp.where(lane == 0, q2, jnp.where(lane == 127, rd_high, 0.0))
    rd_halo = jnp.where((lane == 0) & (rad_index == 0), 0.0, rd_all)
    diagonal = c_mid + c_up + c_low + ax_all + c_right + c_left + rd_all

    def radial_halos(dst):
        even = lax.rem(lane, 2) == 0
        return [jnp.where(even, dst[0, k], rolled(dst[1, k], 126, 1)) for k in range(4)]

    def axial_halo(packed):
        return jnp.where(first_half, rolled(packed, 3, 0), rolled(packed, 5, 0))

    def outside(s, k, axial, radial):
        shift = lax.rem(128 - 2 * s, 128)
        there = axial if k == 0 else rolled(axial, 8 - k, 0)
        return there, rolled(radial[k], shift, 1)

    def inside(x, mid, up, low, right_c, left_c):
        return (
            mid * rolled(x, 4, 0)
            + up * rolled(x, 7, 0)
            + low * rolled(x, 1, 0)
            + right_c * rolled(x, 127, 1)
            + left_c * rolled(x, 1, 1)
        )

    radial1 = radial_halos(rd_dst1)
    keep1 = 0.5 * (1.0 - diagonal)
    half = [0.5 * c for c in (c_mid, c_up, c_low, c_right, c_left)]
    half_ax, half_rd = 0.5 * ax_halo, 0.5 * rd_halo
    half_sigma, half_third = 0.5 * sigma1, 0.5 * third1

    def first_stage(s, carry):
        values = [a_v[k, s] for k in range(4)]
        axial = axial_halo(ax_dst1[s])
        for k in range(4):
            x = values[k]
            ax, rd = outside(s, k, axial, radial1)
            y = keep1 * x + inside(x, *half) + half_ax * ax + half_rd * rd
            y = y + half_sigma * slope(s, k, values, a_v[k, s + 1])
            if k == 3:
                y = y + half_third * sm_v[3, s].astype(F32)
            b_v[k, s] = y
            az_src[0, k, s] = y[0:4]
            az_src[1, k, s] = y[4:8]
        return carry

    lax.fori_loop(0, sections, first_stage, 0)
    up2 = remote(6, az_src.at[1], az_two.at[:, :, 0], above)
    down2 = remote(7, az_src.at[0], az_two.at[:, :, 1], below)
    up2.start()
    down2.start()

    pz.wait_recv()
    az_halo = jnp.where(row < 4, q0, rolled(pz_dst[...], 4, 0))
    half_az = 0.5 * az_halo
    up1.wait_recv()
    down1.wait_recv()
    loads[8].wait()

    def halo_planes(ref, k, s):
        return jnp.concatenate([ref[k, s, 0], ref[k, s, 1]], axis=0)

    def middle_stage(i, carry):
        packs, after, sums = carry
        s = sections - 1 - i
        values = []
        for k in range(4):
            y = b_v[k, s] + half_az * (halo_planes(az_one, k, s) - a_v[k, s])
            b_v[k, s] = y
            values.append(y)
        ax_src2[s] = pack_axial(values)
        packs = pack_radial(s, values, packs)
        sums = source_sums(s, values, after, ss_v, sums)
        return packs, values, sums

    packs, head, sums = lax.fori_loop(
        0, sections, middle_stage, ([zero] * 4, [zero] * 4, (zero, zero))
    )
    for k in range(4):
        rd_src2[k] = packs[k]
    ax2 = remote(8, ax_src2, ax_dst2, other)
    rr2 = remote(9, rd_src2, rd_dst2.at[0], right)
    rl2 = remote(10, rd_src2, rd_dst2.at[1], left)
    ax2.start()
    rr2.start()
    rl2.start()
    sigma2, third2 = source_scalars(sums, head)
    keep2 = 1.0 - (diagonal + az_halo)

    def second_stage(s, carry):
        values = [b_v[k, s] for k in range(4)]
        for k in range(4):
            x = values[k]
            y = keep2 * x + 0.5 * a_v[k, s] + inside(x, c_mid, c_up, c_low, c_right, c_left)
            y = y + sigma2 * slope(s, k, values, b_v[k, s + 1])
            if k == 3:
                y = y + third2 * ss_v[3, s].astype(F32)
            o_v[k, s] = y
        return carry

    lax.fori_loop(0, sections, second_stage, 0)
    rr2.wait_recv()
    rl2.wait_recv()
    radial2 = radial_halos(rd_dst2)
    up2.wait_recv()
    down2.wait_recv()
    ax2.wait_recv()

    def last_stage(s, carry):
        axial = axial_halo(ax_dst2[s])
        for k in range(4):
            ax, rd = outside(s, k, axial, radial2)
            o_v[k, s] = o_v[k, s] + az_halo * halo_planes(az_two, k, s) + ax_halo * ax + rd_halo * rd
        return carry

    lax.fori_loop(0, sections, last_stage, 0)
    store = pltpu.make_async_copy(o_v, out_ref, out_sem)
    store.start()
    for copy in (up1, down1, pz, ax1, rr1, rl1, up2, down2, ax2, rr2, rl2):
        copy.wait_send()
    store.wait()


def shards(
    adjoint_final,
    state_start,
    state_middle,
    speeds,
    flags,
    zones,
    growth_rate,
    transfer_rate,
    nucleation_rate,
):
    dims = adjoint_final.shape
    moms, sections = dims[0], dims[1]
    flat = (moms, sections, 8, 128)
    hbm = pl.BlockSpec(memory_space=pltpu.MemorySpace.HBM)
    vmem = pltpu.VMEM
    dma = pltpu.SemaphoreType.DMA
    out = pl.pallas_call(
        kernel,
        out_shape=jax.ShapeDtypeStruct(flat, F32),
        in_specs=[hbm] * 10,
        out_specs=hbm,
        scratch_shapes=[
            vmem((moms, sections + 1, 8, 128), F32),
            vmem((moms, sections + 1, 8, 128), F32),
            vmem(flat, F32),
            vmem(flat, jnp.bfloat16),
            vmem(flat, jnp.bfloat16),
            vmem((3, 8, 128), F32),
            vmem((3, 8, 128), jnp.int32),
            vmem((8, 128), jnp.int32),
            pltpu.SMEM(growth_rate.shape, F32),
            pltpu.SMEM(transfer_rate.shape, F32),
            pltpu.SMEM(nucleation_rate.shape, F32),
            vmem((8, 128), F32),
            vmem((8, 128), F32),
            vmem((2, moms, sections, 4, 128), F32),
            vmem((moms, sections, 2, 4, 128), F32),
            vmem((moms, sections, 2, 4, 128), F32),
            vmem((sections + 1, 8, 128), F32),
            vmem((sections + 1, 8, 128), F32),
            vmem((sections, 8, 128), F32),
            vmem((sections, 8, 128), F32),
            vmem((5, 8, 128), F32),
            vmem((2, 5, 8, 128), F32),
            vmem((4, 8, 128), F32),
            vmem((2, 4, 8, 128), F32),
            dma((9,)),
            dma((11,)),
            dma((11,)),
            dma,
        ],
        compiler_params=pltpu.CompilerParams(
            collective_id=0, has_side_effects=True, vmem_limit_bytes=40 << 20
        ),
    )(
        adjoint_final,
        adjoint_final.reshape(flat),
        state_middle.reshape(flat),
        state_start.reshape(flat),
        speeds.reshape(3, 8, 128),
        flags.reshape(3, 8, 128),
        zones.reshape(8, 128),
        growth_rate,
        transfer_rate,
        nucleation_rate,
    )
    return out.reshape(dims)


def solution(mesh):
    return jax.shard_map(
        shards,
        mesh=mesh,
        in_specs=(
            P(None, None, "azim", "axial", "rad"),
            P(None, None, "azim", "axial", "rad"),
            P(None, None, "azim", "axial", "rad"),
            P(None, "azim", "axial", "rad"),
            P(None, "azim", "axial", "rad"),
            P("azim", "axial", "rad"),
            P(),
            P(),
            P(),
        ),
        out_specs=P(None, None, "azim", "axial", "rad"),
        check_vma=False,
    )
```

time: 141 us -> 48.9 us (0.35)
  the two profiles are of different devices: /device:TPU:145 before, /device:TPU:1 now
where the time goes in v1:
time: 48.9 us; the launch traced here: 48.2 us
  Pallas kernels  42.1 us (86%)
  local copies, waits for them, and re-layouts  6.11 us (12%)
    pallas_call x1, Pallas kernels, shards(): pl.pallas_call(kernel, out_shape=jax.ShapeDtypeStruct(flat, F32), in_spec...  42.1 us
    unnamed x19, local copies, waits for them, and re-layouts  6.11 us

profile of v1, /device:TPU:1, one launch (start us, length us, event | category | flops | bytes accessed | tf_op | source)
XLA Modules:
  0.0 48.2 jit_solution(12817141359781288082)
XLA Ops:
  0.0 0.0 copy-start.5
  0.0 0.0 copy-start.6
  0.0 0.0 copy-start.7
  0.0 0.0 copy-start.8
  0.0 0.7 %copy-done.5 = s32[2,4,128]{2,1,0:T(4,128)S(1)} copy-done((s32[2,4,128]{2,1,0:T(4,128)S(1)}, s32[2,4,128]{2,1,0:T(4,128)}, u32[]{:S(2)}) %copy-start.5) | copy-done | bytes 4120
  0.7 0.0 copy-done.6
  0.7 0.0 copy-done.7
  0.7 0.0 copy-done.8
  0.7 0.0 copy-start
  0.7 1.1 %copy-done = f32[4,48,2,4,128]{4,3,2,1,0:T(4,128)S(1)} copy-done((f32[4,48,2,4,128]{4,3,2,1,0:T(4,128)S(1)}, f32[4,48,2,4,128]{4,3,2,1,0:T(4,128)}, u32[]{:S(2)}) %copy-start) | copy-done | bytes 786456
  1.8 0.0 copy-start.1
  1.8 1.0 %copy-done.1 = bf16[4,48,2,4,128]{4,3,2,1,0:T(4,128)(2,1)S(1)} copy-done((bf16[4,48,2,4,128]{4,3,2,1,0:T(4,128)(2,1)S(1)}, bf16[4,48,2,4,128]{4,3,2,1,0:T(4,128)(2,1)}, u32[]{:S(2)}) %copy-start.1) | copy-done | bytes 393240
  2.8 0.0 copy-start.2
  2.8 1.0 %copy-done.2 = bf16[4,48,2,4,128]{4,3,2,1,0:T(4,128)(2,1)S(1)} copy-done((bf16[4,48,2,4,128]{4,3,2,1,0:T(4,128)(2,1)S(1)}, bf16[4,48,2,4,128]{4,3,2,1,0:T(4,128)(2,1)}, u32[]{:S(2)}) %copy-start.2) | copy-done | bytes 393240
  3.8 0.0 copy-start.3
  3.8 0.7 %copy-done.3 = f32[3,2,4,128]{3,2,1,0:T(4,128)S(1)} copy-done((f32[3,2,4,128]{3,2,1,0:T(4,128)S(1)}, f32[3,2,4,128]{3,2,1,0:T(4,128)}, u32[]{:S(2)}) %copy-start.3) | copy-done | bytes 12312
  4.5 0.0 copy-start.4
  4.5 0.7 %copy-done.4 = s32[3,2,4,128]{3,2,1,0:T(4,128)S(1)} copy-done((s32[3,2,4,128]{3,2,1,0:T(4,128)S(1)}, s32[3,2,4,128]{3,2,1,0:T(4,128)}, u32[]{:S(2)}) %copy-start.4) | copy-done | bytes 12312
  5.2 42.1 %shard_map.91 = f32[4,48,8,128]{3,2,1,0:T(8,128)S(1)} custom-call(f32[4,48,2,4,128]{4,3,2,1,0:T(4,128)S(1)} %copy-done, f32[4,48,8,128]{3,2,1,0:T(8,128)S(1)} %bitcast.8, bf16[4,48,8,128]{3,2,1,0:T(8,128)(2,1)S(1)} %bitcast.9, bf16[4,48,8,128]{3,2,1,0:T(8,128)(2,1)S(1)} %bitcast.10, f32[3,8,128]{2,1,0:T(8,128)S(1)} %bitcast.11, s32[3,8,128]{2,1,0:T(8,128)S(1)} %bitcast.12, ...), custom_call_target="tpu_custom_call" | custom-call | tf_op jit(solution)/shard_map/pallas_call | solution.py:310
  47.4 0.9 %copy.11 = f32[4,48,2,4,128]{4,3,2,1,0:T(4,128)} copy(f32[4,48,2,4,128]{4,3,2,1,0:T(4,128)S(1)} %bitcast.7) | data formatting | bytes 1572864
Async XLA Ops:
  0.0 0.7 %copy-start.5 = (s32[2,4,128]{2,1,0:T(4,128)S(1)}, s32[2,4,128]{2,1,0:T(4,128)}, u32[]{:S(2)}) copy-start(s32[2,4,128]{2,1,0:T(4,128)} %param.14) | copy-start | bytes 12292
  0.0 0.7 %copy-start.6 = (f32[48]{0:T(128)S(1)}, f32[48]{0:T(128)}, u32[]{:S(2)}) copy-start(f32[48]{0:T(128)} %growth_ref.1) | copy-start | bytes 580
  0.0 0.7 %copy-start.7 = (f32[48]{0:T(128)S(1)}, f32[48]{0:T(128)}, u32[]{:S(2)}) copy-start(f32[48]{0:T(128)} %transfer_ref.1) | copy-start | bytes 580
  0.0 0.7 %copy-start.8 = (f32[4]{0:T(128)S(1)}, f32[4]{0:T(128)}, u32[]{:S(2)}) copy-start(f32[4]{0:T(128)} %nucl_ref.1) | copy-start | bytes 52
  0.7 1.1 %copy-start = (f32[4,48,2,4,128]{4,3,2,1,0:T(4,128)S(1)}, f32[4,48,2,4,128]{4,3,2,1,0:T(4,128)}, u32[]{:S(2)}) copy-start(f32[4,48,2,4,128]{4,3,2,1,0:T(4,128)} %far_ref.1) | copy-start | bytes 2359300
  1.8 1.0 %copy-start.1 = (bf16[4,48,2,4,128]{4,3,2,1,0:T(4,128)(2,1)S(1)}, bf16[4,48,2,4,128]{4,3,2,1,0:T(4,128)(2,1)}, u32[]{:S(2)}) copy-start(bf16[4,48,2,4,128]{4,3,2,1,0:T(4,128)(2,1)} %param.11) | copy-start | bytes 1179652
  2.8 1.0 %copy-start.2 = (bf16[4,48,2,4,128]{4,3,2,1,0:T(4,128)(2,1)S(1)}, bf16[4,48,2,4,128]{4,3,2,1,0:T(4,128)(2,1)}, u32[]{:S(2)}) copy-start(bf16[4,48,2,4,128]{4,3,2,1,0:T(4,128)(2,1)} %param.10) | copy-start | bytes 1179652
  3.8 0.7 %copy-start.3 = (f32[3,2,4,128]{3,2,1,0:T(4,128)S(1)}, f32[3,2,4,128]{3,2,1,0:T(4,128)}, u32[]{:S(2)}) copy-start(f32[3,2,4,128]{3,2,1,0:T(4,128)} %param.12) | copy-start | bytes 36868
  4.5 0.7 %copy-start.4 = (s32[3,2,4,128]{3,2,1,0:T(4,128)S(1)}, s32[3,2,4,128]{3,2,1,0:T(4,128)}, u32[]{:S(2)}) copy-start(s32[3,2,4,128]{3,2,1,0:T(4,128)} %param.13) | copy-start | bytes 36868

commit v2 on v1

--- a/solution.py
+++ b/solution.py
@@ -11,6 +11,7 @@
 crowding = 0.02
 MESH = pl.DeviceIdType.MESH
 F32 = jnp.float32
+UNROLL = 16
 
 
 def rolled(x, shift, axis):
@@ -38,6 +39,9 @@
     other = shifted("axial", 1)
     first_half = lax.axis_index("axial") == 0
 
+    def sweep(step, init):
+        return lax.fori_loop(0, sections, step, init, unroll=UNROLL)
+
     def remote(n, src, dst, device):
         return pltpu.make_async_remote_copy(
             src_ref=src, dst_ref=dst, send_sem=send_sem.at[n], recv_sem=recv_sem.at[n],
@@ -102,7 +106,7 @@
         ax_src1[s] = pack_axial(values)
         return pack_radial(s, values, packs)
 
-    packs = lax.fori_loop(0, sections, pack_first, [zero] * 4)
+    packs = sweep(pack_first, [zero] * 4)
     for k in range(4):
         rd_src1[k] = packs[k]
     ax1 = remote(3, ax_src1, ax_dst1, other)
@@ -148,7 +152,7 @@
         after = [a_v[k, s + 1] for k in range(4)]
         return source_sums(s, values, after, sm_v, sums)
 
-    sums = lax.fori_loop(0, sections, first_sums, (zero, zero))
+    sums = sweep(first_sums, (zero, zero))
     sigma1, third1 = source_scalars(sums, [a_v[k, 0] for k in range(4)])
 
     ax1.wait_recv()
@@ -213,7 +217,7 @@
             az_src[1, k, s] = y[4:8]
         return carry
 
-    lax.fori_loop(0, sections, first_stage, 0)
+    sweep(first_stage, 0)
     up2 = remote(6, az_src.at[1], az_two.at[:, :, 0], above)
     down2 = remote(7, az_src.at[0], az_two.at[:, :, 1], below)
     up2.start()
@@ -242,9 +246,7 @@
         sums = source_sums(s, values, after, ss_v, sums)
         return packs, values, sums
 
-    packs, head, sums = lax.fori_loop(
-        0, sections, middle_stage, ([zero] * 4, [zero] * 4, (zero, zero))
-    )
+    packs, head, sums = sweep(middle_stage, ([zero] * 4, [zero] * 4, (zero, zero)))
     for k in range(4):
         rd_src2[k] = packs[k]
     ax2 = remote(8, ax_src2, ax_dst2, other)
@@ -267,7 +269,7 @@
             o_v[k, s] = y
         return carry
 
-    lax.fori_loop(0, sections, second_stage, 0)
+    sweep(second_stage, 0)
     rr2.wait_recv()
     rl2.wait_recv()
     radial2 = radial_halos(rd_dst2)
@@ -282,7 +284,7 @@
             o_v[k, s] = o_v[k, s] + az_halo * halo_planes(az_two, k, s) + ax_halo * ax + rd_halo * rd
         return carry
 
-    lax.fori_loop(0, sections, last_stage, 0)
+    sweep(last_stage, 0)
     store = pltpu.make_async_copy(o_v, out_ref, out_sem)
     store.start()
     for copy in (up1, down1, pz, ax1, rr1, rl1, up2, down2, ax2, rr2, rl2):
@@ -345,18 +347,21 @@
         compiler_params=pltpu.CompilerParams(
             collective_id=0, has_side_effects=True, vmem_limit_bytes=40 << 20
         ),
-    )(
-        adjoint_final,
-        adjoint_final.reshape(flat),
-        state_middle.reshape(flat),
-        state_start.reshape(flat),
-        speeds.reshape(3, 8, 128),
-        flags.reshape(3, 8, 128),
-        zones.reshape(8, 128),
-        growth_rate,
-        transfer_rate,
-        nucleation_rate,
-    )
+    )(*[
+        pltpu.with_memory_space_constraint(x, pltpu.MemorySpace.HBM)
+        for x in (
+            adjoint_final,
+            adjoint_final.reshape(flat),
+            state_middle.reshape(flat),
+            state_start.reshape(flat),
+            speeds.reshape(3, 8, 128),
+            flags.reshape(3, 8, 128),
+            zones.reshape(8, 128),
+            growth_rate,
+            transfer_rate,
+            nucleation_rate,
+        )
+    ])
     return out.reshape(dims)
 
 

time: 48.9 us -> 36.9 us (0.75)
  Pallas kernels: 42.1 us -> 35.5 us
  local copies, waits for them, and re-layouts: 6.11 us -> 0.88 us
    pallas_call x1, Pallas kernels: 42.1 us -> 35.5 us  [shards(): pl.pallas_call(kernel, out_shape=jax.ShapeDtypeStruct(flat, F32), in_spec...]
    unnamed x19 -> x1, local copies, waits for them, and re-layouts: 6.11 us -> 0.88 us
where the time goes in v2:
time: 36.9 us; the launch traced here: 36.4 us
  Pallas kernels  35.5 us (96%)
  local copies, waits for them, and re-layouts  0.88 us (2%)
    pallas_call x1, Pallas kernels, shards(): pl.pallas_call(kernel, out_shape=jax.ShapeDtypeStruct(flat, F32), in_spec...  35.5 us
    unnamed x1, local copies, waits for them, and re-layouts  0.88 us

profile of v2, /device:TPU:1, one launch (start us, length us, event | category | flops | bytes accessed | tf_op | source)
XLA Modules:
  0.0 36.4 jit_solution(11876156664777184626)
XLA Ops:
  0.0 35.5 %shard_map.91 = f32[4,48,8,128]{3,2,1,0:T(8,128)S(1)} custom-call(f32[4,48,2,4,128]{4,3,2,1,0:T(4,128)} %far_ref.1, f32[4,48,8,128]{3,2,1,0:T(8,128)} %bitcast.8, bf16[4,48,8,128]{3,2,1,0:T(8,128)(2,1)} %bitcast.9, bf16[4,48,8,128]{3,2,1,0:T(8,128)(2,1)} %bitcast.10, f32[3,8,128]{2,1,0:T(8,128)} %bitcast.11, s32[3,8,128]{2,1,0:T(8,128)} %bitcast.12, ...), custom_call_target="tpu_custom_call" | custom-call | tf_op jit(solution)/shard_map/pallas_call | solution.py:312
  35.5 0.9 %copy.11 = f32[4,48,2,4,128]{4,3,2,1,0:T(4,128)} copy(f32[4,48,2,4,128]{4,3,2,1,0:T(4,128)S(1)} %bitcast.7) | data formatting | bytes 1572864

commit v3 on v2

--- a/solution.py
+++ b/solution.py
@@ -11,11 +11,8 @@
 crowding = 0.02
 MESH = pl.DeviceIdType.MESH
 F32 = jnp.float32
-UNROLL = 16
-
-
-def rolled(x, shift, axis):
-    return pltpu.roll(x, shift, axis)
+CHUNKS = 4
+REMOTE = 6 * CHUNKS + 6
 
 
 def shifted(axis, step):
@@ -26,12 +23,12 @@
 def kernel(
     far_ref, af_ref, sm_ref, ss_ref, speeds_ref, flags_ref, zones_ref, growth_ref, transfer_ref, nucl_ref,
     out_ref,
-    a_v, b_v, o_v, sm_v, ss_v, sp_v, fl_v, zn_v, g_s, t_s, n_s,
-    pz_src, pz_dst,
+    a_v, b_v, sm_v, ss_v, sp_v, fl_v, zn_v, g_s, t_s, n_s,
+    pz_src, pz_dst, pa_src, pa_dst,
     az_src, az_one, az_two,
     ax_src1, ax_dst1, ax_src2, ax_dst2,
     rd_src1, rd_dst1, rd_src2, rd_dst2,
-    local_sem, send_sem, recv_sem, out_sem,
+    local_sem, send_sem, recv_sem,
 ):
     sections = sm_ref.shape[1]
     above, below = shifted("azim", 1), shifted("azim", -1)
@@ -39,14 +36,28 @@
     other = shifted("axial", 1)
     first_half = lax.axis_index("axial") == 0
 
-    def sweep(step, init):
-        return lax.fori_loop(0, sections, step, init, unroll=UNROLL)
-
-    def remote(n, src, dst, device):
-        return pltpu.make_async_remote_copy(
+    size = sections // CHUNKS
+    chunks = [pl.ds(c * size, size) for c in reversed(range(CHUNKS))]
+
+    def sweep(step, init, chunk=None):
+        if chunk is None:
+            for chunk in chunks:
+                init = sweep(step, init, chunk)
+            return init
+        top = chunk.start + chunk.size - 1
+        return lax.fori_loop(0, chunk.size, lambda i, c: step(top - i, c), init, unroll=chunk.size)
+
+    sent = []
+
+    def remote(src, dst, device):
+        n = len(sent)
+        copy = pltpu.make_async_remote_copy(
             src_ref=src, dst_ref=dst, send_sem=send_sem.at[n], recv_sem=recv_sem.at[n],
             device_id=device, device_id_type=MESH,
         )
+        copy.start()
+        sent.append(copy)
+        return copy
 
     loads = [
         pltpu.make_async_copy(src, dst, local_sem.at[n])
@@ -63,10 +74,13 @@
         copy.start()
     pl.semaphore_wait(barrier, 5)
 
-    up1 = remote(0, far_ref.at[:, :, 1], az_one.at[:, :, 0], above)
-    down1 = remote(1, far_ref.at[:, :, 0], az_one.at[:, :, 1], below)
-    up1.start()
-    down1.start()
+    planes1 = [
+        (
+            remote(far_ref.at[:, c, 1], az_one.at[:, c, 0], above),
+            remote(far_ref.at[:, c, 0], az_one.at[:, c, 1], below),
+        )
+        for c in chunks
+    ]
 
     row = lax.broadcasted_iota(jnp.int32, (8, 128), 0)
     lane = lax.broadcasted_iota(jnp.int32, (8, 128), 1)
@@ -76,12 +90,12 @@
     def pack_axial(values):
         packed = values[0]
         for k in range(1, 4):
-            packed = jnp.where(arow == lax.rem(edge + k, 4), rolled(values[k], k, 0), packed)
+            packed = jnp.where(arow == lax.rem(edge + k, 4), pltpu.roll(values[k], k, 0), packed)
         return packed
 
     def pack_radial(s, values, packs):
         here = lax.shift_right_logical(lane, 1) == s
-        return [jnp.where(here, rolled(x, 2 * s + 1, 1), pack) for x, pack in zip(values, packs)]
+        return [jnp.where(here, pltpu.roll(x, 2 * s + 1, 1), pack) for x, pack in zip(values, packs)]
 
     zero = jnp.zeros((8, 128), F32)
 
@@ -92,10 +106,10 @@
     p = speeds * upwind
     q = speeds * (1.0 - upwind)
     pz_src[...] = p[0]
-    ax_src1[sections] = p[1]
+    pa_src[...] = p[1]
     rd_src1[4] = p[2]
-    pz = remote(2, pz_src, pz_dst, below)
-    pz.start()
+    pz = remote(pz_src, pz_dst, below)
+    pa = remote(pa_src, pa_dst, other)
 
     loads[2].wait()
     a_v[:, sections] = jnp.zeros((4, 8, 128), F32)
@@ -106,15 +120,16 @@
         ax_src1[s] = pack_axial(values)
         return pack_radial(s, values, packs)
 
-    packs = sweep(pack_first, [zero] * 4)
+    packs, rows1 = [zero] * 4, []
+    for c in chunks:
+        packs = sweep(pack_first, packs, c)
+        rows1.append(remote(ax_src1.at[c], ax_dst1.at[c], other))
     for k in range(4):
         rd_src1[k] = packs[k]
-    ax1 = remote(3, ax_src1, ax_dst1, other)
-    rr1 = remote(4, rd_src1, rd_dst1.at[0], right)
-    rl1 = remote(5, rd_src1, rd_dst1.at[1], left)
-    ax1.start()
-    rr1.start()
-    rl1.start()
+    lanes1 = (
+        remote(rd_src1, rd_dst1.at[0], right),
+        remote(rd_src1, rd_dst1.at[1], left),
+    )
 
     for copy in loads[3:7]:
         copy.wait()
@@ -155,45 +170,45 @@
     sums = sweep(first_sums, (zero, zero))
     sigma1, third1 = source_scalars(sums, [a_v[k, 0] for k in range(4)])
 
-    ax1.wait_recv()
-    rr1.wait_recv()
-    rl1.wait_recv()
+    pa.wait_recv()
+    for copy in lanes1:
+        copy.wait_recv()
     p0, p1, p2 = p[0], p[1], p[2]
     q0, q1, q2 = q[0], q[1], q[2]
-    c_mid = jnp.where(row < 4, rolled(p0, 4, 0), q0)
-    c_up = jnp.where(arow < 3, rolled(p1, 7, 0), 0.0)
+    c_mid = jnp.where(row < 4, pltpu.roll(p0, 4, 0), q0)
+    c_up = jnp.where(arow < 3, pltpu.roll(p1, 7, 0), 0.0)
     c_low = jnp.where(arow > 0, q1, 0.0)
-    far_face = jnp.where(first_half, rolled(ax_dst1[sections], 3, 0), 0.0)
+    far_face = jnp.where(first_half, pltpu.roll(pa_dst[...], 3, 0), 0.0)
     ax_all = jnp.where(arow == 0, q1, jnp.where(arow == 3, far_face, 0.0))
     ax_halo = jnp.where(arow == edge, ax_all, 0.0)
-    c_right = jnp.where(lane < 127, rolled(p2, 127, 1), 0.0)
+    c_right = jnp.where(lane < 127, pltpu.roll(p2, 127, 1), 0.0)
     c_left = jnp.where(lane > 0, q2, 0.0)
     rad_index = lax.axis_index("rad")
     rad_last = lax.axis_size("rad") - 1
-    rd_high = jnp.where(rad_index < rad_last, rolled(rd_dst1[1, 4], 127, 1), 0.0)
+    rd_high = jnp.where(rad_index < rad_last, pltpu.roll(rd_dst1[1, 4], 127, 1), 0.0)
     rd_all = jnp.where(lane == 0, q2, jnp.where(lane == 127, rd_high, 0.0))
     rd_halo = jnp.where((lane == 0) & (rad_index == 0), 0.0, rd_all)
     diagonal = c_mid + c_up + c_low + ax_all + c_right + c_left + rd_all
 
     def radial_halos(dst):
         even = lax.rem(lane, 2) == 0
-        return [jnp.where(even, dst[0, k], rolled(dst[1, k], 126, 1)) for k in range(4)]
+        return [jnp.where(even, dst[0, k], pltpu.roll(dst[1, k], 126, 1)) for k in range(4)]
 
     def axial_halo(packed):
-        return jnp.where(first_half, rolled(packed, 3, 0), rolled(packed, 5, 0))
+        return jnp.where(first_half, pltpu.roll(packed, 3, 0), pltpu.roll(packed, 5, 0))
 
     def outside(s, k, axial, radial):
         shift = lax.rem(128 - 2 * s, 128)
-        there = axial if k == 0 else rolled(axial, 8 - k, 0)
-        return there, rolled(radial[k], shift, 1)
+        there = axial if k == 0 else pltpu.roll(axial, 8 - k, 0)
+        return there, pltpu.roll(radial[k], shift, 1)
 
     def inside(x, mid, up, low, right_c, left_c):
         return (
-            mid * rolled(x, 4, 0)
-            + up * rolled(x, 7, 0)
-            + low * rolled(x, 1, 0)
-            + right_c * rolled(x, 127, 1)
-            + left_c * rolled(x, 1, 1)
+            mid * pltpu.roll(x, 4, 0)
+            + up * pltpu.roll(x, 7, 0)
+            + low * pltpu.roll(x, 1, 0)
+            + right_c * pltpu.roll(x, 127, 1)
+            + left_c * pltpu.roll(x, 1, 1)
         )
 
     radial1 = radial_halos(rd_dst1)
@@ -217,25 +232,25 @@
             az_src[1, k, s] = y[4:8]
         return carry
 
-    sweep(first_stage, 0)
-    up2 = remote(6, az_src.at[1], az_two.at[:, :, 0], above)
-    down2 = remote(7, az_src.at[0], az_two.at[:, :, 1], below)
-    up2.start()
-    down2.start()
+    planes2 = []
+    for c, rows in zip(chunks, rows1):
+        rows.wait_recv()
+        sweep(first_stage, 0, c)
+        planes2.append((
+            remote(az_src.at[1, :, c], az_two.at[:, c, 0], above),
+            remote(az_src.at[0, :, c], az_two.at[:, c, 1], below),
+        ))
 
     pz.wait_recv()
-    az_halo = jnp.where(row < 4, q0, rolled(pz_dst[...], 4, 0))
+    az_halo = jnp.where(row < 4, q0, pltpu.roll(pz_dst[...], 4, 0))
     half_az = 0.5 * az_halo
-    up1.wait_recv()
-    down1.wait_recv()
     loads[8].wait()
 
     def halo_planes(ref, k, s):
         return jnp.concatenate([ref[k, s, 0], ref[k, s, 1]], axis=0)
 
-    def middle_stage(i, carry):
+    def middle_stage(s, carry):
         packs, after, sums = carry
-        s = sections - 1 - i
         values = []
         for k in range(4):
             y = b_v[k, s] + half_az * (halo_planes(az_one, k, s) - a_v[k, s])
@@ -246,15 +261,19 @@
         sums = source_sums(s, values, after, ss_v, sums)
         return packs, values, sums
 
-    packs, head, sums = sweep(middle_stage, ([zero] * 4, [zero] * 4, (zero, zero)))
+    carry, rows2 = ([zero] * 4, [zero] * 4, (zero, zero)), []
+    for c, planes in zip(chunks, planes1):
+        for copy in planes:
+            copy.wait_recv()
+        carry = sweep(middle_stage, carry, c)
+        rows2.append(remote(ax_src2.at[c], ax_dst2.at[c], other))
+    packs, head, sums = carry
     for k in range(4):
         rd_src2[k] = packs[k]
-    ax2 = remote(8, ax_src2, ax_dst2, other)
-    rr2 = remote(9, rd_src2, rd_dst2.at[0], right)
-    rl2 = remote(10, rd_src2, rd_dst2.at[1], left)
-    ax2.start()
-    rr2.start()
-    rl2.start()
+    lanes2 = (
+        remote(rd_src2, rd_dst2.at[0], right),
+        remote(rd_src2, rd_dst2.at[1], left),
+    )
     sigma2, third2 = source_scalars(sums, head)
     keep2 = 1.0 - (diagonal + az_halo)
 
@@ -266,30 +285,27 @@
             y = y + sigma2 * slope(s, k, values, b_v[k, s + 1])
             if k == 3:
                 y = y + third2 * ss_v[3, s].astype(F32)
-            o_v[k, s] = y
+            out_ref[k, s] = y
         return carry
 
     sweep(second_stage, 0)
-    rr2.wait_recv()
-    rl2.wait_recv()
+    for copy in lanes2:
+        copy.wait_recv()
     radial2 = radial_halos(rd_dst2)
-    up2.wait_recv()
-    down2.wait_recv()
-    ax2.wait_recv()
 
     def last_stage(s, carry):
         axial = axial_halo(ax_dst2[s])
         for k in range(4):
             ax, rd = outside(s, k, axial, radial2)
-            o_v[k, s] = o_v[k, s] + az_halo * halo_planes(az_two, k, s) + ax_halo * ax + rd_halo * rd
+            out_ref[k, s] = out_ref[k, s] + az_halo * halo_planes(az_two, k, s) + ax_halo * ax + rd_halo * rd
         return carry
 
-    sweep(last_stage, 0)
-    store = pltpu.make_async_copy(o_v, out_ref, out_sem)
-    store.start()
-    for copy in (up1, down1, pz, ax1, rr1, rl1, up2, down2, ax2, rr2, rl2):
+    for c, planes, rows in zip(chunks, planes2, rows2):
+        for copy in (*planes, rows):
+            copy.wait_recv()
+        sweep(last_stage, 0, c)
+    for copy in sent:
         copy.wait_send()
-    store.wait()
 
 
 def shards(
@@ -313,11 +329,10 @@
         kernel,
         out_shape=jax.ShapeDtypeStruct(flat, F32),
         in_specs=[hbm] * 10,
-        out_specs=hbm,
+        out_specs=pl.BlockSpec(memory_space=pltpu.VMEM),
         scratch_shapes=[
             vmem((moms, sections + 1, 8, 128), F32),
             vmem((moms, sections + 1, 8, 128), F32),
-            vmem(flat, F32),
             vmem(flat, jnp.bfloat16),
             vmem(flat, jnp.bfloat16),
             vmem((3, 8, 128), F32),
@@ -328,11 +343,13 @@
             pltpu.SMEM(nucleation_rate.shape, F32),
             vmem((8, 128), F32),
             vmem((8, 128), F32),
+            vmem((8, 128), F32),
+            vmem((8, 128), F32),
             vmem((2, moms, sections, 4, 128), F32),
             vmem((moms, sections, 2, 4, 128), F32),
             vmem((moms, sections, 2, 4, 128), F32),
-            vmem((sections + 1, 8, 128), F32),
-            vmem((sections + 1, 8, 128), F32),
+            vmem((sections, 8, 128), F32),
+            vmem((sections, 8, 128), F32),
             vmem((sections, 8, 128), F32),
             vmem((sections, 8, 128), F32),
             vmem((5, 8, 128), F32),
@@ -340,9 +357,8 @@
             vmem((4, 8, 128), F32),
             vmem((2, 4, 8, 128), F32),
             dma((9,)),
-            dma((11,)),
-            dma((11,)),
-            dma,
+            dma((REMOTE,)),
+            dma((REMOTE,)),
         ],
         compiler_params=pltpu.CompilerParams(
             collective_id=0, has_side_effects=True, vmem_limit_bytes=40 << 20

time: 36.9 us -> 34.5 us (0.935); the launches traced: 36.4 us -> 34.5 us
  Pallas kernels: 35.5 us -> 33.6 us
    pallas_call x1, Pallas kernels: 35.5 us -> 33.6 us  [shards(): pl.pallas_call(kernel, out_shape=jax.ShapeDtypeStruct(flat, F32), in_spec...]
where the time goes in v3:
time: 34.5 us
  Pallas kernels  33.6 us (97%)
  local copies, waits for them, and re-layouts  0.88 us (3%)
    pallas_call x1, Pallas kernels, shards(): pl.pallas_call(kernel, out_shape=jax.ShapeDtypeStruct(flat, F32), in_spec...  33.6 us
    unnamed x1, local copies, waits for them, and re-layouts  0.88 us

profile of v3, /device:TPU:1, one launch (start us, length us, event | category | flops | bytes accessed | tf_op | source)
XLA Modules:
  0.0 34.5 jit_solution(285253994551740829)
XLA Ops:
  0.0 33.6 %shard_map.91 = f32[4,48,8,128]{3,2,1,0:T(8,128)S(1)} custom-call(f32[4,48,2,4,128]{4,3,2,1,0:T(4,128)} %far_ref.1, f32[4,48,8,128]{3,2,1,0:T(8,128)} %bitcast.8, bf16[4,48,8,128]{3,2,1,0:T(8,128)(2,1)} %bitcast.9, bf16[4,48,8,128]{3,2,1,0:T(8,128)(2,1)} %bitcast.10, f32[3,8,128]{2,1,0:T(8,128)} %bitcast.11, s32[3,8,128]{2,1,0:T(8,128)} %bitcast.12, ...), custom_call_target="tpu_custom_call" | custom-call | tf_op jit(solution)/shard_map/pallas_call | solution.py:328
  33.6 0.9 %copy.11 = f32[4,48,2,4,128]{4,3,2,1,0:T(4,128)} copy(f32[4,48,2,4,128]{4,3,2,1,0:T(4,128)S(1)} %bitcast.7) | data formatting | bytes 1572864

commit v4 on v3

--- a/solution.py
+++ b/solution.py
@@ -12,6 +12,10 @@
 MESH = pl.DeviceIdType.MESH
 F32 = jnp.float32
 CHUNKS = 4
+HOLD = 2
+EARLY = 3
+EARLY_TWO = 2
+HOLD2 = 4
 REMOTE = 6 * CHUNKS + 6
 
 
@@ -47,15 +51,20 @@
         top = chunk.start + chunk.size - 1
         return lax.fori_loop(0, chunk.size, lambda i, c: step(top - i, c), init, unroll=chunk.size)
 
-    sent = []
-
-    def remote(src, dst, device):
+    sent, held = [], []
+    place = lax.rem(lax.axis_index("azim"), 4)
+
+    def remote(src, dst, device, hold=None):
         n = len(sent)
         copy = pltpu.make_async_remote_copy(
             src_ref=src, dst_ref=dst, send_sem=send_sem.at[n], recv_sem=recv_sem.at[n],
             device_id=device, device_id_type=MESH,
         )
-        copy.start()
+        if hold is None:
+            copy.start()
+        else:
+            pl.when(jnp.logical_not(hold))(copy.start)
+            held.append((hold, copy))
         sent.append(copy)
         return copy
 
@@ -76,8 +85,8 @@
 
     planes1 = [
         (
-            remote(far_ref.at[:, c, 1], az_one.at[:, c, 0], above),
-            remote(far_ref.at[:, c, 0], az_one.at[:, c, 1], below),
+            remote(far_ref.at[:, c, 1], az_one.at[:, c, 0], above, place == 1),
+            remote(far_ref.at[:, c, 0], az_one.at[:, c, 1], below, place == 2),
         )
         for c in chunks
     ]
@@ -130,6 +139,17 @@
         remote(rd_src1, rd_dst1.at[0], right),
         remote(rd_src1, rd_dst1.at[1], left),
     )
+
+    waits = rows1[:HOLD]
+    late = (place == 1) | (place == 2)
+
+    @pl.when(late)
+    def _():
+        for copy in waits:
+            copy.wait_send()
+
+    for hold, copy in held:
+        pl.when(hold)(copy.start)
 
     for copy in loads[3:7]:
         copy.wait()
@@ -197,10 +217,11 @@
     def axial_halo(packed):
         return jnp.where(first_half, pltpu.roll(packed, 3, 0), pltpu.roll(packed, 5, 0))
 
-    def outside(s, k, axial, radial):
-        shift = lax.rem(128 - 2 * s, 128)
-        there = axial if k == 0 else pltpu.roll(axial, 8 - k, 0)
-        return there, pltpu.roll(radial[k], shift, 1)
+    def row_halo(k, axial):
+        return axial if k == 0 else pltpu.roll(axial, 8 - k, 0)
+
+    def radial_halo(s, k, radial):
+        return pltpu.roll(radial[k], lax.rem(128 - 2 * s, 128), 1)
 
     def inside(x, mid, up, low, right_c, left_c):
         return (
@@ -222,7 +243,7 @@
         axial = axial_halo(ax_dst1[s])
         for k in range(4):
             x = values[k]
-            ax, rd = outside(s, k, axial, radial1)
+            ax, rd = row_halo(k, axial), radial_halo(s, k, radial1)
             y = keep1 * x + inside(x, *half) + half_ax * ax + half_rd * rd
             y = y + half_sigma * slope(s, k, values, a_v[k, s + 1])
             if k == 3:
@@ -233,12 +254,19 @@
         return carry
 
     planes2 = []
+    held.clear()
+
+    def later(chunk, one_link, two_links):
+        n = [chunk is c for c in chunks].index(True)
+        hold = [place == p for p, early in ((one_link, EARLY), (two_links, EARLY_TWO)) if n >= early]
+        return functools.reduce(jnp.logical_or, hold) if hold else None
+
     for c, rows in zip(chunks, rows1):
         rows.wait_recv()
         sweep(first_stage, 0, c)
         planes2.append((
-            remote(az_src.at[1, :, c], az_two.at[:, c, 0], above),
-            remote(az_src.at[0, :, c], az_two.at[:, c, 1], below),
+            remote(az_src.at[1, :, c], az_two.at[:, c, 0], above, later(c, 1, 3)),
+            remote(az_src.at[0, :, c], az_two.at[:, c, 1], below, later(c, 2, 0)),
         ))
 
     pz.wait_recv()
@@ -293,19 +321,42 @@
         copy.wait_recv()
     radial2 = radial_halos(rd_dst2)
 
-    def last_stage(s, carry):
+    def add_lanes(s, carry):
+        for k in range(4):
+            out_ref[k, s] = out_ref[k, s] + rd_halo * radial_halo(s, k, radial2)
+        return carry
+
+    def add_planes(s, carry):
+        for k in range(4):
+            out_ref[k, s] = out_ref[k, s] + az_halo * halo_planes(az_two, k, s)
+        return carry
+
+    def add_rows(s, carry):
         axial = axial_halo(ax_dst2[s])
         for k in range(4):
-            ax, rd = outside(s, k, axial, radial2)
-            out_ref[k, s] = out_ref[k, s] + az_halo * halo_planes(az_two, k, s) + ax_halo * ax + rd_halo * rd
+            out_ref[k, s] = out_ref[k, s] + ax_halo * row_halo(k, axial)
         return carry
 
+    sweep(add_lanes, 0)
+
+    for copy in rows2[:HOLD2]:
+        copy.wait_send()
+    for hold, copy in held:
+        pl.when(hold)(copy.start)
+
     for c, planes, rows in zip(chunks, planes2, rows2):
-        for copy in (*planes, rows):
+        for copy in planes:
             copy.wait_recv()
-        sweep(last_stage, 0, c)
+        sweep(add_planes, 0, c)
+        rows.wait_recv()
+        sweep(add_rows, 0, c)
     for copy in sent:
-        copy.wait_send()
+        if any(copy is w for w in rows2[:HOLD2]):
+            continue
+        if any(copy is w for w in waits):
+            pl.when(jnp.logical_not(late))(copy.wait_send)
+        else:
+            copy.wait_send()
 
 
 def shards(

time: 34.5 us -> 33.2 us (0.962)
  Pallas kernels: 33.6 us -> 32.2 us
    pallas_call x1, Pallas kernels: 33.6 us -> 32.2 us  [shards(): pl.pallas_call(kernel, out_shape=jax.ShapeDtypeStruct(flat, F32), in_spec...]
where the time goes in v4:
time: 33.2 us; the launch traced here: 33.1 us
  Pallas kernels  32.2 us (97%)
  local copies, waits for them, and re-layouts  0.88 us (3%)
    pallas_call x1, Pallas kernels, shards(): pl.pallas_call(kernel, out_shape=jax.ShapeDtypeStruct(flat, F32), in_spec...  32.2 us
    unnamed x1, local copies, waits for them, and re-layouts  0.88 us

profile of v4, /device:TPU:1, one launch (start us, length us, event | category | flops | bytes accessed | tf_op | source)
XLA Modules:
  0.0 33.1 jit_solution(4805709127371798413)
XLA Ops:
  0.0 32.2 %shard_map.91 = f32[4,48,8,128]{3,2,1,0:T(8,128)S(1)} custom-call(f32[4,48,2,4,128]{4,3,2,1,0:T(4,128)} %far_ref.1, f32[4,48,8,128]{3,2,1,0:T(8,128)} %bitcast.8, bf16[4,48,8,128]{3,2,1,0:T(8,128)(2,1)} %bitcast.9, bf16[4,48,8,128]{3,2,1,0:T(8,128)(2,1)} %bitcast.10, f32[3,8,128]{2,1,0:T(8,128)} %bitcast.11, s32[3,8,128]{2,1,0:T(8,128)} %bitcast.12, ...), custom_call_target="tpu_custom_call" | custom-call | tf_op jit(solution)/shard_map/pallas_call | solution.py:379
  32.2 0.9 %copy.11 = f32[4,48,2,4,128]{4,3,2,1,0:T(4,128)} copy(f32[4,48,2,4,128]{4,3,2,1,0:T(4,128)S(1)} %bitcast.7) | data formatting | bytes 1572864

commit v5 on v4

--- a/solution.py
+++ b/solution.py
@@ -11,11 +11,11 @@
 crowding = 0.02
 MESH = pl.DeviceIdType.MESH
 F32 = jnp.float32
-CHUNKS = 4
-HOLD = 2
-EARLY = 3
+CHUNKS = 3
+HOLD = 1
+EARLY = 2
 EARLY_TWO = 2
-HOLD2 = 4
+HOLD2 = 3
 REMOTE = 6 * CHUNKS + 6
 
 

time: 33.2 us -> 32.9 us (level)
  no operation moved by 1% of the time
where the time goes in v5:
time: 32.9 us
  Pallas kernels  32 us (97%)
  local copies, waits for them, and re-layouts  0.88 us (3%)
    pallas_call x1, Pallas kernels, shards(): pl.pallas_call(kernel, out_shape=jax.ShapeDtypeStruct(flat, F32), in_spec...  32 us
    unnamed x1, local copies, waits for them, and re-layouts  0.88 us

profile of v5, /device:TPU:1, one launch (start us, length us, event | category | flops | bytes accessed | tf_op | source)
XLA Modules:
  0.0 32.9 jit_solution(15691418555361178883)
XLA Ops:
  0.0 32.0 %shard_map.91 = f32[4,48,8,128]{3,2,1,0:T(8,128)S(1)} custom-call(f32[4,48,2,4,128]{4,3,2,1,0:T(4,128)} %far_ref.1, f32[4,48,8,128]{3,2,1,0:T(8,128)} %bitcast.8, bf16[4,48,8,128]{3,2,1,0:T(8,128)(2,1)} %bitcast.9, bf16[4,48,8,128]{3,2,1,0:T(8,128)(2,1)} %bitcast.10, f32[3,8,128]{2,1,0:T(8,128)} %bitcast.11, s32[3,8,128]{2,1,0:T(8,128)} %bitcast.12, ...), custom_call_target="tpu_custom_call" | custom-call | tf_op jit(solution)/shard_map/pallas_call | solution.py:379
  32.0 0.9 %copy.11 = f32[4,48,2,4,128]{4,3,2,1,0:T(4,128)} copy(f32[4,48,2,4,128]{4,3,2,1,0:T(4,128)S(1)} %bitcast.7) | data formatting | bytes 1572864

commit v6 on v5

--- a/solution.py
+++ b/solution.py
@@ -15,7 +15,7 @@
 HOLD = 1
 EARLY = 2
 EARLY_TWO = 2
-HOLD2 = 3
+HOLD2 = 2
 REMOTE = 6 * CHUNKS + 6
 
 

time: 32.9 us -> 33 us (level)
  no operation moved by 1% of the time
where the time goes in v6:
time: 33 us; the launch traced here: 32.9 us
  Pallas kernels  32 us (97%)
  local copies, waits for them, and re-layouts  0.88 us (3%)
    pallas_call x1, Pallas kernels, shards(): pl.pallas_call(kernel, out_shape=jax.ShapeDtypeStruct(flat, F32), in_spec...  32 us
    unnamed x1, local copies, waits for them, and re-layouts  0.88 us

profile of v6, /device:TPU:1, one launch (start us, length us, event | category | flops | bytes accessed | tf_op | source)
XLA Modules:
  0.0 32.9 jit_solution(12988483137755820128)
XLA Ops:
  0.0 32.0 %shard_map.91 = f32[4,48,8,128]{3,2,1,0:T(8,128)S(1)} custom-call(f32[4,48,2,4,128]{4,3,2,1,0:T(4,128)} %far_ref.1, f32[4,48,8,128]{3,2,1,0:T(8,128)} %bitcast.8, bf16[4,48,8,128]{3,2,1,0:T(8,128)(2,1)} %bitcast.9, bf16[4,48,8,128]{3,2,1,0:T(8,128)(2,1)} %bitcast.10, f32[3,8,128]{2,1,0:T(8,128)} %bitcast.11, s32[3,8,128]{2,1,0:T(8,128)} %bitcast.12, ...), custom_call_target="tpu_custom_call" | custom-call | tf_op jit(solution)/shard_map/pallas_call | solution.py:379
  32.0 0.9 %copy.11 = f32[4,48,2,4,128]{4,3,2,1,0:T(4,128)} copy(f32[4,48,2,4,128]{4,3,2,1,0:T(4,128)S(1)} %bitcast.7) | data formatting | bytes 1572864

commit v7 on v6

--- a/solution.py
+++ b/solution.py
@@ -77,7 +77,7 @@
         ])
     ]
     barrier = pltpu.get_barrier_semaphore()
-    for device in (above, below, right, left, other):
+    for device in (other, above, below, right, left):
         pl.semaphore_signal(barrier, inc=1, device_id=device, device_id_type=MESH)
     for copy in loads:
         copy.start()

time: 33 us -> 33 us (level)
  no operation moved by 1% of the time
where the time goes in v7:
time: 33 us; the launch traced here: 32.9 us
  Pallas kernels  32 us (97%)
  local copies, waits for them, and re-layouts  0.88 us (3%)
    pallas_call x1, Pallas kernels, shards(): pl.pallas_call(kernel, out_shape=jax.ShapeDtypeStruct(flat, F32), in_spec...  32 us
    unnamed x1, local copies, waits for them, and re-layouts  0.88 us

profile of v7, /device:TPU:1, one launch (start us, length us, event | category | flops | bytes accessed | tf_op | source)
XLA Modules:
  0.0 32.9 jit_solution(16001900145189544211)
XLA Ops:
  0.0 32.0 %shard_map.91 = f32[4,48,8,128]{3,2,1,0:T(8,128)S(1)} custom-call(f32[4,48,2,4,128]{4,3,2,1,0:T(4,128)} %far_ref.1, f32[4,48,8,128]{3,2,1,0:T(8,128)} %bitcast.8, bf16[4,48,8,128]{3,2,1,0:T(8,128)(2,1)} %bitcast.9, bf16[4,48,8,128]{3,2,1,0:T(8,128)(2,1)} %bitcast.10, f32[3,8,128]{2,1,0:T(8,128)} %bitcast.11, s32[3,8,128]{2,1,0:T(8,128)} %bitcast.12, ...), custom_call_target="tpu_custom_call" | custom-call | tf_op jit(solution)/shard_map/pallas_call | solution.py:379
  32.0 0.9 %copy.11 = f32[4,48,2,4,128]{4,3,2,1,0:T(4,128)} copy(f32[4,48,2,4,128]{4,3,2,1,0:T(4,128)S(1)} %bitcast.7) | data formatting | bytes 1572864
